TPU v7x, 512 devices: a whole 4x4x16 slice. The times are simulated.
512 devices in a mesh: gx: 32 (over z, core), gy: 4 (over y), gz: 4 (over x).
Axes of the slice: x: 4, y: 4, z: 16, core: 2. Of those that a mesh axis runs over, the one named last changes fastest.
Arguments:
- right_side: float32 [512, 256, 512], P('gx', 'gy', 'gz'), may hold values from -18 to 18
- inv_density: float32 [512, 256, 512], P('gx', 'gy', 'gz'), may hold values from 0.5 to 2
- active: int32 [512, 256, 512], P('gx', 'gy', 'gz'), may hold values 0 or 1
Outputs:
- solution_field: float32 [512, 256, 512], P('gx', 'gy', 'gz')
- residual: float32 [512, 256, 512], P('gx', 'gy', 'gz')
All inputs are finite; a program needn't handle non-finite values. No bound on the sum of `active` on one device may be relied on, other than what follows from the above.
Results may differ from a plain program's by a relative error of at most 0.0003.
Values sent between devices are 32-bit elements; how exact they have to be, the bound alone decides.
A program may use at most 64 MiB of HBM per device.

v0:
```python
import jax
import jax.numpy as jnp
from jax import lax
from jax.sharding import PartitionSpec as P

STEPS = 6


basis_shift = 7.0
basis_scale = 7.0
NEIGHBOURS = ((2, 1, 1), (0, 1, 1), (1, 2, 1), (1, 0, 1), (1, 1, 2), (1, 1, 0))


def extended(cells, sides, width):
    for axis, dim in sides:
        count = lax.axis_size(axis)
        ends = count - 1
        head = lax.slice_in_dim(cells, 0, width, axis=dim)
        tail = lax.slice_in_dim(cells, cells.shape[dim] - width, cells.shape[dim], axis=dim)
        cells = jnp.concatenate(
            [
                lax.ppermute(tail, axis, [(i, (i + 1) % count) for i in range(ends)]),
                cells,
                lax.ppermute(head, axis, [((i + 1) % count, i) for i in range(ends)]),
            ],
            axis=dim,
        )
    return cells


def shifted(field, offset):
    extent = field.shape
    return field[
        offset[0] : extent[0] - 2 + offset[0],
        offset[1] : extent[1] - 2 + offset[1],
        offset[2] : extent[2] - 2 + offset[2],
    ]


def face_table(weight_pad):
    center_weight = shifted(weight_pad, (1, 1, 1))
    diagonal = jnp.zeros_like(center_weight)
    faces = []
    for offset in NEIGHBOURS:
        other_weight = shifted(weight_pad, offset)
        liquid_side = other_weight > 0.0
        denominator = jnp.where(liquid_side, center_weight + other_weight, 1.0)
        face_value = jnp.where(
            liquid_side, 2.0 * center_weight * other_weight / denominator, center_weight
        )
        diagonal = diagonal + face_value
        faces.append(face_value)
    return (faces, diagonal)


def apply_faces(vector_pad, faces, diagonal):
    center_value = shifted(vector_pad, (1, 1, 1))
    beside = jnp.zeros_like(center_value)
    for offset, face_value in zip(NEIGHBOURS, faces):
        beside = beside + face_value * shifted(vector_pad, offset)
    return diagonal * center_value - beside


def next_basis(image_field, previous):
    return (image_field - basis_shift * previous) / basis_scale


def least_squares(triangle):
    column_count = triangle.shape[1] - 1
    row_ids = lax.broadcasted_iota(jnp.int32, (column_count + 1, column_count), 0)
    col_ids = lax.broadcasted_iota(jnp.int32, (column_count + 1, column_count), 1)
    change = jnp.where(row_ids == col_ids, basis_shift, 0.0) + jnp.where(
        row_ids == col_ids + 1, basis_scale, 0.0
    )
    change = change.astype(triangle.dtype)
    hess = jnp.dot(triangle, change, precision=lax.Precision.HIGHEST)
    target = triangle[:, 0]
    for pivot_index in range(column_count):
        first_value = hess[pivot_index, pivot_index]
        second_value = hess[pivot_index + 1, pivot_index]
        radius = jnp.sqrt(first_value * first_value + second_value * second_value)
        cosine = first_value / radius
        sine_value = second_value / radius
        upper_row = cosine * hess[pivot_index] + sine_value * hess[pivot_index + 1]
        lower_row = cosine * hess[pivot_index + 1] - sine_value * hess[pivot_index]
        hess = hess.at[pivot_index].set(upper_row).at[pivot_index + 1].set(lower_row)
        upper_target = cosine * target[pivot_index] + sine_value * target[pivot_index + 1]
        lower_target = cosine * target[pivot_index + 1] - sine_value * target[pivot_index]
        target = target.at[pivot_index].set(upper_target).at[pivot_index + 1].set(lower_target)
    solved = [None] * column_count
    for row_index in reversed(range(column_count)):
        running = target[row_index]
        for column_index in range(row_index + 1, column_count):
            running = running - hess[row_index, column_index] * solved[column_index]
        solved[row_index] = running / hess[row_index, row_index]
    coefficients = jnp.stack(solved)
    first_unit = jnp.where(
        lax.broadcasted_iota(jnp.int32, (column_count + 1,), 0) == 0, 1.0, 0.0
    ).astype(triangle.dtype)
    leftover = first_unit - jnp.dot(change, coefficients, precision=lax.Precision.HIGHEST)
    return (coefficients, leftover)


def on_device(right_side, inv_density, active):
    liquid = active.astype(jnp.float32)
    weight = inv_density * liquid
    vector = right_side * liquid
    basis_list = [vector]
    vector_pad, weight_pad = (
        extended(vector, (("gx", 0), ("gy", 1), ("gz", 2)), 1),
        extended(weight, (("gx", 0), ("gy", 1), ("gz", 2)), 1),
    )
    faces, diagonal = face_table(weight_pad)
    current = next_basis(apply_faces(vector_pad, faces, diagonal), vector)
    basis_list.append(current)
    for power_index in range(STEPS - 1):
        current_pad = extended(current, (("gx", 0), ("gy", 1), ("gz", 2)), 1)
        current = next_basis(apply_faces(current_pad, faces, diagonal), current)
        basis_list.append(current)
    stacked = jnp.stack(basis_list).reshape(STEPS + 1, -1)
    local_gram = jnp.dot(stacked, stacked.T, precision=lax.Precision.HIGHEST)
    gram_matrix = lax.psum(local_gram, ("gx", "gy", "gz"))
    triangle = jnp.linalg.cholesky(gram_matrix).T
    coefficients, leftover = least_squares(triangle)
    solution_field = jnp.zeros_like(right_side)
    for power_index in range(STEPS):
        solution_field = solution_field + coefficients[power_index] * basis_list[power_index]
    residual = jnp.zeros_like(right_side)
    for power_index in range(STEPS + 1):
        residual = residual + leftover[power_index] * basis_list[power_index]
    return (solution_field, residual)


def solution(mesh):
    placed = (P("gx", "gy", "gz"), P("gx", "gy", "gz"), P("gx", "gy", "gz"))
    return jax.shard_map(
        on_device,
        mesh=mesh,
        in_specs=placed,
        out_specs=(P("gx", "gy", "gz"), P("gx", "gy", "gz")),
        check_vma=False,
    )
```

profile of v0, /device:TPU:1, one launch (start us, length us, event | category | flops | bytes accessed | tf_op | source)
XLA Modules:
  0.0 420.3 jit_solution(13076338501270926982)
XLA Ops:
  0.6 1.5 convert_multiply_fusion
  2.1 8.7 %collective-permute-start = (f32[1,64,128]{2,1,0:T(8,128)S(1)}, f32[1,64,128]{2,1,0:T(8,128)S(1)}, u32[]{:S(2)}, u32[]{:S(2)}) collective-permute-start(f32[1,64,128]{2,1,0:T(8,128)S(1)} %get-tuple-element.343), channel_id=1, source_target_pairs={{16,0},{32,16},{48,32},{64,48},{80,64},{96,80},{112,96},{128,112},... | collective-permute-start | bytes 98312 | tf_op jit(solution)/shard_map/ppermute | solution.py:24
  10.9 1.9 collective-permute-start.1
  12.8 2.4 collective-permute-start.6
  15.2 3.2 collective-permute-start.7
  19.8 4.0 collective-permute-start.3
  25.1 4.0 collective-permute-start.9
  31.3 4.0 collective-permute-start.5
  37.4 4.0 collective-permute-start.11
  45.3 5.5 %broadcast_multiply_fusion.5 = (f32[16,64,128]{2,1,0:T(8,128)S(1)}, f32[16,64,128]{2,1,0:T(8,128)}, f32[16,64,128]{2,1,0:T(8,128)S(1)}, f32[16,64,128]{2,1,0:T(8,128)S(1)}) fusion(f32[16,64,128]{2,1,0:T(8,128)S(1)} %get-tuple-element.345, f32[18,1,128]{2,1,0:T(1,128)S(1)} %collective-permute-done.8, f32[1,64,128]{2,1,0:T(8,128)S(1)} %collective-permute-done.6, ...), kind=kLoop, calls=%fused_computation.242 | loop fusion | flops 12320768 | bytes 3332672 | tf_op jit(solution)/shard_map/div | solution.py:65
  50.8 3.4 collective-permute-start.12
  54.2 2.7 collective-permute-start.13
  59.3 4.0 collective-permute-start.15
  65.2 1.3 copy.21
  68.1 4.0 collective-permute-start.17
  74.5 4.5 %broadcast_multiply_fusion.4 = (f32[16,64,128]{2,1,0:T(8,128)S(1)}, f32[16,64,128]{2,1,0:T(8,128)}) fusion(f32[16,64,128]{2,1,0:T(8,128)} %get-tuple-element.301, f32[16,64,128]{2,1,0:T(8,128)S(1)} %get-tuple-element.303, f32[18,1,128]{2,1,0:T(1,128)S(1)} %collective-permute-done.14, f32[1,64,128]{2,1,0:T(8,128)S(1)} %collective-permute-done.12, ...), kind=kLoop, calls=%fused_computation.241 | loop fusion | flops 9306112 | bytes 3847456 | tf_op jit(solution)/shard_map/div | solution.py:65
  79.0 3.4 collective-permute-start.18
  82.4 4.7 %collective-permute-start.19 = (f32[1,64,128]{2,1,0:T(8,128)S(1)}, f32[1,64,128]{2,1,0:T(8,128)S(1)}, u32[]{:S(2)}, u32[]{:S(2)}) collective-permute-start(f32[1,64,128]{2,1,0:T(8,128)S(1)} %get-tuple-element.338), channel_id=1, source_target_pairs={{0,16},{16,32},{32,48},{48,64},{64,80},{80,96},{96,112},{112,128},... | collective-permute-start | bytes 98312 | tf_op jit(solution)/shard_map/ppermute | solution.py:22
  89.4 4.5 %collective-permute-start.21 = (f32[18,1,128]{2,1,0:T(1,128)S(1)}, f32[18,1,128]{2,1,0:T(1,128)S(1)}, u32[]{:S(2)}, u32[]{:S(2)}) collective-permute-start(f32[18,1,128]{2,1,0:T(1,128)S(1)} %get-tuple-element.324), channel_id=1, source_target_pairs={{0,4},{4,8},{8,12},{1,5},{5,9},{9,13},{2,6},{6,10},{10,14},{3,7},{... | collective-permute-start | bytes 27656 | tf_op jit(solution)/shard_map/ppermute | solution.py:22
  96.1 1.3 copy.25
  98.7 1.3 copy.27
  100.1 4.6 %collective-permute-start.23 = (f32[18,66,1]{1,2,0:T(1,128)S(1)}, f32[18,66,1]{1,2,0:T(1,128)S(1)}, u32[]{:S(2)}, u32[]{:S(2)}) collective-permute-start(f32[18,66,1]{1,2,0:T(1,128)S(1)} %copy.27), channel_id=1, source_target_pairs={{0,1},{1,2},{2,3},{4,5},{5,6},{6,7},{8,9},{9,10},{10,11},{12,13},{... | collective-permute-start | bytes 14264 | tf_op jit(solution)/shard_map/ppermute | solution.py:22
  107.0 4.5 %broadcast_multiply_fusion.3 = (f32[16,64,128]{2,1,0:T(8,128)S(1)}, f32[16,64,128]{2,1,0:T(8,128)}) fusion(f32[16,64,128]{2,1,0:T(8,128)} %get-tuple-element.299, f32[16,64,128]{2,1,0:T(8,128)S(1)} %get-tuple-element.303, f32[18,1,128]{2,1,0:T(1,128)S(1)} %collective-permute-done.20, f32[1,64,128]{2,1,0:T(8,128)S(1)} %collective-permute-done.18, ...), kind=kLoop, calls=%fused_computation.240 | loop fusion | flops 9306112 | bytes 3847456 | tf_op jit(solution)/shard_map/div | solution.py:65
  111.6 1.9 collective-permute-start.24
  113.5 5.5 %collective-permute-start.25 = (f32[1,64,128]{2,1,0:T(8,128)S(1)}, f32[1,64,128]{2,1,0:T(8,128)S(1)}, u32[]{:S(2)}, u32[]{:S(2)}) collective-permute-start(f32[1,64,128]{2,1,0:T(8,128)S(1)} %get-tuple-element.336), channel_id=1, source_target_pairs={{0,16},{16,32},{32,48},{48,64},{64,80},{80,96},{96,112},{112,128},... | collective-permute-start | bytes 98312 | tf_op jit(solution)/shard_map/ppermute | solution.py:22
  121.4 4.5 %collective-permute-start.27 = (f32[18,1,128]{2,1,0:T(1,128)S(1)}, f32[18,1,128]{2,1,0:T(1,128)S(1)}, u32[]{:S(2)}, u32[]{:S(2)}) collective-permute-start(f32[18,1,128]{2,1,0:T(1,128)S(1)} %get-tuple-element.322), channel_id=1, source_target_pairs={{0,4},{4,8},{8,12},{1,5},{5,9},{9,13},{2,6},{6,10},{10,14},{3,7},{... | collective-permute-start | bytes 27656 | tf_op jit(solution)/shard_map/ppermute | solution.py:22
  128.1 1.3 copy.29
  130.7 1.3 copy.31
  132.1 4.7 %collective-permute-start.29 = (f32[18,66,1]{1,2,0:T(1,128)S(1)}, f32[18,66,1]{1,2,0:T(1,128)S(1)}, u32[]{:S(2)}, u32[]{:S(2)}) collective-permute-start(f32[18,66,1]{1,2,0:T(1,128)S(1)} %copy.31), channel_id=1, source_target_pairs={{0,1},{1,2},{2,3},{4,5},{5,6},{6,7},{8,9},{9,10},{10,11},{12,13},{... | collective-permute-start | bytes 14264 | tf_op jit(solution)/shard_map/ppermute | solution.py:22
  139.2 6.2 %broadcast_multiply_fusion.2 = (f32[16,64,128]{2,1,0:T(8,128)S(1)}, f32[16,64,128]{2,1,0:T(8,128)}) fusion(f32[16,64,128]{2,1,0:T(8,128)} %get-tuple-element.297, f32[16,64,128]{2,1,0:T(8,128)S(1)} %get-tuple-element.303, f32[18,1,128]{2,1,0:T(1,128)S(1)} %collective-permute-done.26, f32[1,64,128]{2,1,0:T(8,128)S(1)} %collective-permute-done.24, ...), kind=kLoop, calls=%fused_computation.239 | loop fusion | flops 9306112 | bytes 3847456 | tf_op jit(solution)/shard_map/div | solution.py:65
  145.4 1.9 collective-permute-start.30
  147.3 5.4 %collective-permute-start.31 = (f32[1,64,128]{2,1,0:T(8,128)S(1)}, f32[1,64,128]{2,1,0:T(8,128)S(1)}, u32[]{:S(2)}, u32[]{:S(2)}) collective-permute-start(f32[1,64,128]{2,1,0:T(8,128)S(1)} %get-tuple-element.334), channel_id=1, source_target_pairs={{0,16},{16,32},{32,48},{48,64},{64,80},{80,96},{96,112},{112,128},... | collective-permute-start | bytes 98312 | tf_op jit(solution)/shard_map/ppermute | solution.py:22
  155.0 4.5 %collective-permute-start.33 = (f32[18,1,128]{2,1,0:T(1,128)S(1)}, f32[18,1,128]{2,1,0:T(1,128)S(1)}, u32[]{:S(2)}, u32[]{:S(2)}) collective-permute-start(f32[18,1,128]{2,1,0:T(1,128)S(1)} %get-tuple-element.320), channel_id=1, source_target_pairs={{0,4},{4,8},{8,12},{1,5},{5,9},{9,13},{2,6},{6,10},{10,14},{3,7},{... | collective-permute-start | bytes 27656 | tf_op jit(solution)/shard_map/ppermute | solution.py:22
  161.7 1.3 copy.33
  164.3 1.3 copy.35
  165.7 4.6 %collective-permute-start.35 = (f32[18,66,1]{1,2,0:T(1,128)S(1)}, f32[18,66,1]{1,2,0:T(1,128)S(1)}, u32[]{:S(2)}, u32[]{:S(2)}) collective-permute-start(f32[18,66,1]{1,2,0:T(1,128)S(1)} %copy.35), channel_id=1, source_target_pairs={{0,1},{1,2},{2,3},{4,5},{5,6},{6,7},{8,9},{9,10},{10,11},{12,13},{... | collective-permute-start | bytes 14264 | tf_op jit(solution)/shard_map/ppermute | solution.py:22
  172.6 6.4 %broadcast_multiply_fusion.1 = (f32[16,64,128]{2,1,0:T(8,128)S(1)}, f32[16,64,128]{2,1,0:T(8,128)}) fusion(f32[16,64,128]{2,1,0:T(8,128)} %get-tuple-element.295, f32[16,64,128]{2,1,0:T(8,128)S(1)} %get-tuple-element.303, f32[18,1,128]{2,1,0:T(1,128)S(1)} %collective-permute-done.32, f32[1,64,128]{2,1,0:T(8,128)S(1)} %collective-permute-done.30, ...), kind=kLoop, calls=%fused_computation.238 | loop fusion | flops 9306112 | bytes 3847456 | tf_op jit(solution)/shard_map/div | solution.py:65
  179.1 1.9 collective-permute-start.36
  181.0 5.5 %collective-permute-start.37 = (f32[1,64,128]{2,1,0:T(8,128)S(1)}, f32[1,64,128]{2,1,0:T(8,128)S(1)}, u32[]{:S(2)}, u32[]{:S(2)}) collective-permute-start(f32[1,64,128]{2,1,0:T(8,128)S(1)} %get-tuple-element.332), channel_id=1, source_target_pairs={{0,16},{16,32},{32,48},{48,64},{64,80},{80,96},{96,112},{112,128},... | collective-permute-start | bytes 98312 | tf_op jit(solution)/shard_map/ppermute | solution.py:22
  188.9 4.5 %collective-permute-start.39 = (f32[18,1,128]{2,1,0:T(1,128)S(1)}, f32[18,1,128]{2,1,0:T(1,128)S(1)}, u32[]{:S(2)}, u32[]{:S(2)}) collective-permute-start(f32[18,1,128]{2,1,0:T(1,128)S(1)} %get-tuple-element.318), channel_id=1, source_target_pairs={{0,4},{4,8},{8,12},{1,5},{5,9},{9,13},{2,6},{6,10},{10,14},{3,7},{... | collective-permute-start | bytes 27656 | tf_op jit(solution)/shard_map/ppermute | solution.py:22
  195.6 1.3 copy.37
  198.2 1.3 copy.39
  199.6 4.6 %collective-permute-start.41 = (f32[18,66,1]{1,2,0:T(1,128)S(1)}, f32[18,66,1]{1,2,0:T(1,128)S(1)}, u32[]{:S(2)}, u32[]{:S(2)}) collective-permute-start(f32[18,66,1]{1,2,0:T(1,128)S(1)} %copy.39), channel_id=1, source_target_pairs={{0,1},{1,2},{2,3},{4,5},{5,6},{6,7},{8,9},{9,10},{10,11},{12,13},{... | collective-permute-start | bytes 14264 | tf_op jit(solution)/shard_map/ppermute | solution.py:22
  206.5 6.4 %broadcast_multiply_fusion = (f32[16,64,128]{2,1,0:T(8,128)}, f32[16,64,128]{2,1,0:T(8,128)}) fusion(f32[16,64,128]{2,1,0:T(8,128)} %get-tuple-element.293, f32[16,64,128]{2,1,0:T(8,128)S(1)} %get-tuple-element.303, f32[18,1,128]{2,1,0:T(1,128)S(1)} %collective-permute-done.38, f32[1,64,128]{2,1,0:T(8,128)S(1)} %collective-permute-done.36, ...), kind=kLoop, calls=%fused_computation.237 | loop fusion | flops 9306112 | bytes 3847456 | tf_op jit(solution)/shard_map/div | solution.py:65
  212.9 11.1 %stack.52 = f32[7,16,64,128]{3,0,2,1:T(8,128)} concatenate(f32[1,16,64,128]{3,0,2,1:T(1,128)S(1)} %bitcast.98, f32[1,16,64,128]{3,0,2,1:T(1,128)S(1)} %bitcast.99, f32[1,16,64,128]{3,0,2,1:T(1,128)S(1)} %bitcast.100, f32[1,16,64,128]{3,0,2,1:T(1,128)} %bitcast.101, f32[1,16,64,128]{3,0,2,1:T(1,128)} %bitcast.102, f32[1,16,64,128]{3,0,2,1:T(1,128)} %bitcast.103, ...), dimensions={0} | concatenate | bytes 7340032 | tf_op jit(solution)/shard_map/stack | solution.py:120
  224.0 12.7 %convolution_bitcast_fusion = f32[7,7]{0,1:T(8,128)S(1)} fusion(f32[7,16,64,128]{3,0,2,1:T(8,128)} %stack.52), kind=kOutput, calls=%fused_computation | convolution fusion | flops 77070336 | bytes 3670212 | tf_op jit(solution)/shard_map/dot_general | solution.py:121
  236.7 116.9 %psum.7 = f32[7,7]{0,1:T(8,128)S(1)} all-reduce(f32[7,7]{0,1:T(8,128)S(1)} %convolution_bitcast_fusion), channel_id=1, replica_groups=mesh['gx'=32,'gy'=4,'gz'=4] {'gx','gy','gz'}, use_global_device_ids=true, to_apply=%region_0.1 | all-reduce | flops 49 | bytes 392 | tf_op jit(solution)/shard_map/psum | solution.py:122
  417.5 2.8 multiply_add_fusion
  (165 shorter events, 66.9 us)
Async XLA Ops:
  2.1 16.3 %collective-permute-start = (f32[1,64,128]{2,1,0:T(8,128)S(1)}, f32[1,64,128]{2,1,0:T(8,128)S(1)}, u32[]{:S(2)}, u32[]{:S(2)}) collective-permute-start(f32[1,64,128]{2,1,0:T(8,128)S(1)} %get-tuple-element.343), channel_id=1, source_target_pairs={{16,0},{32,16},{48,32},{64,48},{80,64},{96,80},{112,96},{128,112},... | collective-permute-start | bytes 98312 | tf_op jit(solution)/shard_map/ppermute | solution.py:24
  10.9 7.5 %collective-permute-start.1 = (f32[1,64,128]{2,1,0:T(8,128)S(1)}, f32[1,64,128]{2,1,0:T(8,128)S(1)}, u32[]{:S(2)}, u32[]{:S(2)}) collective-permute-start(f32[1,64,128]{2,1,0:T(8,128)S(1)} %get-tuple-element.342), channel_id=1, source_target_pairs={{0,16},{16,32},{32,48},{48,64},{64,80},{80,96},{96,112},{112,128},... | collective-permute-start | bytes 98312 | tf_op jit(solution)/shard_map/ppermute | solution.py:22
  12.8 10.9 %collective-permute-start.6 = (f32[1,64,128]{2,1,0:T(8,128)S(1)}, f32[1,64,128]{2,1,0:T(8,128)S(1)}, u32[]{:S(2)}, u32[]{:S(2)}) collective-permute-start(f32[1,64,128]{2,1,0:T(8,128)S(1)} %get-tuple-element.347), channel_id=1, source_target_pairs={{16,0},{32,16},{48,32},{64,48},{80,64},{96,80},{112,96},{128,112},... | collective-permute-start | bytes 98312 | tf_op jit(solution)/shard_map/ppermute | solution.py:24
  15.2 8.5 %collective-permute-start.7 = (f32[1,64,128]{2,1,0:T(8,128)S(1)}, f32[1,64,128]{2,1,0:T(8,128)S(1)}, u32[]{:S(2)}, u32[]{:S(2)}) collective-permute-start(f32[1,64,128]{2,1,0:T(8,128)S(1)} %get-tuple-element.346), channel_id=1, source_target_pairs={{0,16},{16,32},{32,48},{48,64},{64,80},{80,96},{96,112},{112,128},... | collective-permute-start | bytes 98312 | tf_op jit(solution)/shard_map/ppermute | solution.py:22
  18.5 10.6 %collective-permute-start.2 = (f32[18,1,128]{2,1,0:T(1,128)S(1)}, f32[18,1,128]{2,1,0:T(1,128)S(1)}, u32[]{:S(2)}, u32[]{:S(2)}) collective-permute-start(f32[18,1,128]{2,1,0:T(1,128)S(1)} %get-tuple-element.328), channel_id=1, source_target_pairs={{4,0},{8,4},{12,8},{5,1},{9,5},{13,9},{6,2},{10,6},{14,10},{7,3},{... | collective-permute-start | bytes 27656 | tf_op jit(solution)/shard_map/ppermute | solution.py:24
  19.8 9.3 %collective-permute-start.3 = (f32[18,1,128]{2,1,0:T(1,128)S(1)}, f32[18,1,128]{2,1,0:T(1,128)S(1)}, u32[]{:S(2)}, u32[]{:S(2)}) collective-permute-start(f32[18,1,128]{2,1,0:T(1,128)S(1)} %get-tuple-element.329), channel_id=1, source_target_pairs={{0,4},{4,8},{8,12},{1,5},{5,9},{9,13},{2,6},{6,10},{10,14},{3,7},{... | collective-permute-start | bytes 27656 | tf_op jit(solution)/shard_map/ppermute | solution.py:22
  23.8 11.5 %collective-permute-start.8 = (f32[18,1,128]{2,1,0:T(1,128)S(1)}, f32[18,1,128]{2,1,0:T(1,128)S(1)}, u32[]{:S(2)}, u32[]{:S(2)}) collective-permute-start(f32[18,1,128]{2,1,0:T(1,128)S(1)} %get-tuple-element.331), channel_id=1, source_target_pairs={{4,0},{8,4},{12,8},{5,1},{9,5},{13,9},{6,2},{10,6},{14,10},{7,3},{... | collective-permute-start | bytes 27656 | tf_op jit(solution)/shard_map/ppermute | solution.py:24
  25.1 10.2 %collective-permute-start.9 = (f32[18,1,128]{2,1,0:T(1,128)S(1)}, f32[18,1,128]{2,1,0:T(1,128)S(1)}, u32[]{:S(2)}, u32[]{:S(2)}) collective-permute-start(f32[18,1,128]{2,1,0:T(1,128)S(1)} %get-tuple-element.330), channel_id=1, source_target_pairs={{0,4},{4,8},{8,12},{1,5},{5,9},{9,13},{2,6},{6,10},{10,14},{3,7},{... | collective-permute-start | bytes 27656 | tf_op jit(solution)/shard_map/ppermute | solution.py:22
  29.7 11.8 %collective-permute-start.4 = (f32[18,66,1]{1,2,0:T(1,128)S(1)}, f32[18,66,1]{1,2,0:T(1,128)S(1)}, u32[]{:S(2)}, u32[]{:S(2)}) collective-permute-start(f32[18,66,1]{1,2,0:T(1,128)S(1)} %copy.13), channel_id=1, source_target_pairs={{1,0},{2,1},{3,2},{5,4},{6,5},{7,6},{9,8},{10,9},{11,10},{13,12},{... | collective-permute-start | bytes 14264 | tf_op jit(solution)/shard_map/ppermute | solution.py:24
  31.3 10.5 %collective-permute-start.5 = (f32[18,66,1]{1,2,0:T(1,128)S(1)}, f32[18,66,1]{1,2,0:T(1,128)S(1)}, u32[]{:S(2)}, u32[]{:S(2)}) collective-permute-start(f32[18,66,1]{1,2,0:T(1,128)S(1)} %copy.15), channel_id=1, source_target_pairs={{0,1},{1,2},{2,3},{4,5},{5,6},{6,7},{8,9},{9,10},{10,11},{12,13},{... | collective-permute-start | bytes 14264 | tf_op jit(solution)/shard_map/ppermute | solution.py:22
  35.9 7.1 %collective-permute-start.10 = (f32[18,66,1]{1,2,0:T(1,128)S(1)}, f32[18,66,1]{1,2,0:T(1,128)S(1)}, u32[]{:S(2)}, u32[]{:S(2)}) collective-permute-start(f32[18,66,1]{1,2,0:T(1,128)S(1)} %copy.17), channel_id=1, source_target_pairs={{1,0},{2,1},{3,2},{5,4},{6,5},{7,6},{9,8},{10,9},{11,10},{13,12},{... | collective-permute-start | bytes 14264 | tf_op jit(solution)/shard_map/ppermute | solution.py:24
  37.4 6.7 %collective-permute-start.11 = (f32[18,66,1]{1,2,0:T(1,128)S(1)}, f32[18,66,1]{1,2,0:T(1,128)S(1)}, u32[]{:S(2)}, u32[]{:S(2)}) collective-permute-start(f32[18,66,1]{1,2,0:T(1,128)S(1)} %copy.19), channel_id=1, source_target_pairs={{0,1},{1,2},{2,3},{4,5},{5,6},{6,7},{8,9},{9,10},{10,11},{12,13},{... | collective-permute-start | bytes 14264 | tf_op jit(solution)/shard_map/ppermute | solution.py:22
  50.8 6.1 %collective-permute-start.12 = (f32[1,64,128]{2,1,0:T(8,128)S(1)}, f32[1,64,128]{2,1,0:T(8,128)S(1)}, u32[]{:S(2)}, u32[]{:S(2)}) collective-permute-start(f32[1,64,128]{2,1,0:T(8,128)S(1)} %get-tuple-element.341), channel_id=1, source_target_pairs={{16,0},{32,16},{48,32},{64,48},{80,64},{96,80},{112,96},{128,112},... | collective-permute-start | bytes 98312 | tf_op jit(solution)/shard_map/ppermute | solution.py:24
  54.2 3.7 collective-permute-start.13
  58.0 5.3 %collective-permute-start.14 = (f32[18,1,128]{2,1,0:T(1,128)S(1)}, f32[18,1,128]{2,1,0:T(1,128)S(1)}, u32[]{:S(2)}, u32[]{:S(2)}) collective-permute-start(f32[18,1,128]{2,1,0:T(1,128)S(1)} %get-tuple-element.327), channel_id=1, source_target_pairs={{4,0},{8,4},{12,8},{5,1},{9,5},{13,9},{6,2},{10,6},{14,10},{7,3},{... | collective-permute-start | bytes 27656 | tf_op jit(solution)/shard_map/ppermute | solution.py:24
  59.3 4.8 %collective-permute-start.15 = (f32[18,1,128]{2,1,0:T(1,128)S(1)}, f32[18,1,128]{2,1,0:T(1,128)S(1)}, u32[]{:S(2)}, u32[]{:S(2)}) collective-permute-start(f32[18,1,128]{2,1,0:T(1,128)S(1)} %get-tuple-element.326), channel_id=1, source_target_pairs={{0,4},{4,8},{8,12},{1,5},{5,9},{9,13},{2,6},{6,10},{10,14},{3,7},{... | collective-permute-start | bytes 27656 | tf_op jit(solution)/shard_map/ppermute | solution.py:22
  66.5 5.6 %collective-permute-start.16 = (f32[18,66,1]{1,2,0:T(1,128)S(1)}, f32[18,66,1]{1,2,0:T(1,128)S(1)}, u32[]{:S(2)}, u32[]{:S(2)}) collective-permute-start(f32[18,66,1]{1,2,0:T(1,128)S(1)} %copy.21), channel_id=1, source_target_pairs={{1,0},{2,1},{3,2},{5,4},{6,5},{7,6},{9,8},{10,9},{11,10},{13,12},{... | collective-permute-start | bytes 14264 | tf_op jit(solution)/shard_map/ppermute | solution.py:24
  68.1 5.2 %collective-permute-start.17 = (f32[18,66,1]{1,2,0:T(1,128)S(1)}, f32[18,66,1]{1,2,0:T(1,128)S(1)}, u32[]{:S(2)}, u32[]{:S(2)}) collective-permute-start(f32[18,66,1]{1,2,0:T(1,128)S(1)} %copy.23), channel_id=1, source_target_pairs={{0,1},{1,2},{2,3},{4,5},{5,6},{6,7},{8,9},{9,10},{10,11},{12,13},{... | collective-permute-start | bytes 14264 | tf_op jit(solution)/shard_map/ppermute | solution.py:22
  79.0 8.0 %collective-permute-start.18 = (f32[1,64,128]{2,1,0:T(8,128)S(1)}, f32[1,64,128]{2,1,0:T(8,128)S(1)}, u32[]{:S(2)}, u32[]{:S(2)}) collective-permute-start(f32[1,64,128]{2,1,0:T(8,128)S(1)} %get-tuple-element.339), channel_id=1, source_target_pairs={{16,0},{32,16},{48,32},{64,48},{80,64},{96,80},{112,96},{128,112},... | collective-permute-start | bytes 98312 | tf_op jit(solution)/shard_map/ppermute | solution.py:24
  82.4 5.7 %collective-permute-start.19 = (f32[1,64,128]{2,1,0:T(8,128)S(1)}, f32[1,64,128]{2,1,0:T(8,128)S(1)}, u32[]{:S(2)}, u32[]{:S(2)}) collective-permute-start(f32[1,64,128]{2,1,0:T(8,128)S(1)} %get-tuple-element.338), channel_id=1, source_target_pairs={{0,16},{16,32},{32,48},{48,64},{64,80},{80,96},{96,112},{112,128},... | collective-permute-start | bytes 98312 | tf_op jit(solution)/shard_map/ppermute | solution.py:22
  88.1 5.8 %collective-permute-start.20 = (f32[18,1,128]{2,1,0:T(1,128)S(1)}, f32[18,1,128]{2,1,0:T(1,128)S(1)}, u32[]{:S(2)}, u32[]{:S(2)}) collective-permute-start(f32[18,1,128]{2,1,0:T(1,128)S(1)} %get-tuple-element.325), channel_id=1, source_target_pairs={{4,0},{8,4},{12,8},{5,1},{9,5},{13,9},{6,2},{10,6},{14,10},{7,3},{... | collective-permute-start | bytes 27656 | tf_op jit(solution)/shard_map/ppermute | solution.py:24
  89.4 5.3 %collective-permute-start.21 = (f32[18,1,128]{2,1,0:T(1,128)S(1)}, f32[18,1,128]{2,1,0:T(1,128)S(1)}, u32[]{:S(2)}, u32[]{:S(2)}) collective-permute-start(f32[18,1,128]{2,1,0:T(1,128)S(1)} %get-tuple-element.324), channel_id=1, source_target_pairs={{0,4},{4,8},{8,12},{1,5},{5,9},{9,13},{2,6},{6,10},{10,14},{3,7},{... | collective-permute-start | bytes 27656 | tf_op jit(solution)/shard_map/ppermute | solution.py:22
  97.4 7.2 %collective-permute-start.22 = (f32[18,66,1]{1,2,0:T(1,128)S(1)}, f32[18,66,1]{1,2,0:T(1,128)S(1)}, u32[]{:S(2)}, u32[]{:S(2)}) collective-permute-start(f32[18,66,1]{1,2,0:T(1,128)S(1)} %copy.25), channel_id=1, source_target_pairs={{1,0},{2,1},{3,2},{5,4},{6,5},{7,6},{9,8},{10,9},{11,10},{13,12},{... | collective-permute-start | bytes 14264 | tf_op jit(solution)/shard_map/ppermute | solution.py:24
  100.1 5.7 %collective-permute-start.23 = (f32[18,66,1]{1,2,0:T(1,128)S(1)}, f32[18,66,1]{1,2,0:T(1,128)S(1)}, u32[]{:S(2)}, u32[]{:S(2)}) collective-permute-start(f32[18,66,1]{1,2,0:T(1,128)S(1)} %copy.27), channel_id=1, source_target_pairs={{0,1},{1,2},{2,3},{4,5},{5,6},{6,7},{8,9},{9,10},{10,11},{12,13},{... | collective-permute-start | bytes 14264 | tf_op jit(solution)/shard_map/ppermute | solution.py:22
  111.6 7.5 %collective-permute-start.24 = (f32[1,64,128]{2,1,0:T(8,128)S(1)}, f32[1,64,128]{2,1,0:T(8,128)S(1)}, u32[]{:S(2)}, u32[]{:S(2)}) collective-permute-start(f32[1,64,128]{2,1,0:T(8,128)S(1)} %get-tuple-element.337), channel_id=1, source_target_pairs={{16,0},{32,16},{48,32},{64,48},{80,64},{96,80},{112,96},{128,112},... | collective-permute-start | bytes 98312 | tf_op jit(solution)/shard_map/ppermute | solution.py:24
  113.5 6.6 %collective-permute-start.25 = (f32[1,64,128]{2,1,0:T(8,128)S(1)}, f32[1,64,128]{2,1,0:T(8,128)S(1)}, u32[]{:S(2)}, u32[]{:S(2)}) collective-permute-start(f32[1,64,128]{2,1,0:T(8,128)S(1)} %get-tuple-element.336), channel_id=1, source_target_pairs={{0,16},{16,32},{32,48},{48,64},{64,80},{80,96},{96,112},{112,128},... | collective-permute-start | bytes 98312 | tf_op jit(solution)/shard_map/ppermute | solution.py:22
  120.1 5.8 %collective-permute-start.26 = (f32[18,1,128]{2,1,0:T(1,128)S(1)}, f32[18,1,128]{2,1,0:T(1,128)S(1)}, u32[]{:S(2)}, u32[]{:S(2)}) collective-permute-start(f32[18,1,128]{2,1,0:T(1,128)S(1)} %get-tuple-element.323), channel_id=1, source_target_pairs={{4,0},{8,4},{12,8},{5,1},{9,5},{13,9},{6,2},{10,6},{14,10},{7,3},{... | collective-permute-start | bytes 27656 | tf_op jit(solution)/shard_map/ppermute | solution.py:24
  121.4 5.3 %collective-permute-start.27 = (f32[18,1,128]{2,1,0:T(1,128)S(1)}, f32[18,1,128]{2,1,0:T(1,128)S(1)}, u32[]{:S(2)}, u32[]{:S(2)}) collective-permute-start(f32[18,1,128]{2,1,0:T(1,128)S(1)} %get-tuple-element.322), channel_id=1, source_target_pairs={{0,4},{4,8},{8,12},{1,5},{5,9},{9,13},{2,6},{6,10},{10,14},{3,7},{... | collective-permute-start | bytes 27656 | tf_op jit(solution)/shard_map/ppermute | solution.py:22
  129.4 7.4 %collective-permute-start.28 = (f32[18,66,1]{1,2,0:T(1,128)S(1)}, f32[18,66,1]{1,2,0:T(1,128)S(1)}, u32[]{:S(2)}, u32[]{:S(2)}) collective-permute-start(f32[18,66,1]{1,2,0:T(1,128)S(1)} %copy.29), channel_id=1, source_target_pairs={{1,0},{2,1},{3,2},{5,4},{6,5},{7,6},{9,8},{10,9},{11,10},{13,12},{... | collective-permute-start | bytes 14264 | tf_op jit(solution)/shard_map/ppermute | solution.py:24
  132.1 5.9 %collective-permute-start.29 = (f32[18,66,1]{1,2,0:T(1,128)S(1)}, f32[18,66,1]{1,2,0:T(1,128)S(1)}, u32[]{:S(2)}, u32[]{:S(2)}) collective-permute-start(f32[18,66,1]{1,2,0:T(1,128)S(1)} %copy.31), channel_id=1, source_target_pairs={{0,1},{1,2},{2,3},{4,5},{5,6},{6,7},{8,9},{9,10},{10,11},{12,13},{... | collective-permute-start | bytes 14264 | tf_op jit(solution)/shard_map/ppermute | solution.py:22
  145.4 7.3 %collective-permute-start.30 = (f32[1,64,128]{2,1,0:T(8,128)S(1)}, f32[1,64,128]{2,1,0:T(8,128)S(1)}, u32[]{:S(2)}, u32[]{:S(2)}) collective-permute-start(f32[1,64,128]{2,1,0:T(8,128)S(1)} %get-tuple-element.335), channel_id=1, source_target_pairs={{16,0},{32,16},{48,32},{64,48},{80,64},{96,80},{112,96},{128,112},... | collective-permute-start | bytes 98312 | tf_op jit(solution)/shard_map/ppermute | solution.py:24
  147.3 6.4 %collective-permute-start.31 = (f32[1,64,128]{2,1,0:T(8,128)S(1)}, f32[1,64,128]{2,1,0:T(8,128)S(1)}, u32[]{:S(2)}, u32[]{:S(2)}) collective-permute-start(f32[1,64,128]{2,1,0:T(8,128)S(1)} %get-tuple-element.334), channel_id=1, source_target_pairs={{0,16},{16,32},{32,48},{48,64},{64,80},{80,96},{96,112},{112,128},... | collective-permute-start | bytes 98312 | tf_op jit(solution)/shard_map/ppermute | solution.py:22
  153.7 5.8 %collective-permute-start.32 = (f32[18,1,128]{2,1,0:T(1,128)S(1)}, f32[18,1,128]{2,1,0:T(1,128)S(1)}, u32[]{:S(2)}, u32[]{:S(2)}) collective-permute-start(f32[18,1,128]{2,1,0:T(1,128)S(1)} %get-tuple-element.321), channel_id=1, source_target_pairs={{4,0},{8,4},{12,8},{5,1},{9,5},{13,9},{6,2},{10,6},{14,10},{7,3},{... | collective-permute-start | bytes 27656 | tf_op jit(solution)/shard_map/ppermute | solution.py:24
  155.0 5.3 %collective-permute-start.33 = (f32[18,1,128]{2,1,0:T(1,128)S(1)}, f32[18,1,128]{2,1,0:T(1,128)S(1)}, u32[]{:S(2)}, u32[]{:S(2)}) collective-permute-start(f32[18,1,128]{2,1,0:T(1,128)S(1)} %get-tuple-element.320), channel_id=1, source_target_pairs={{0,4},{4,8},{8,12},{1,5},{5,9},{9,13},{2,6},{6,10},{10,14},{3,7},{... | collective-permute-start | bytes 27656 | tf_op jit(solution)/shard_map/ppermute | solution.py:22
  163.0 7.2 %collective-permute-start.34 = (f32[18,66,1]{1,2,0:T(1,128)S(1)}, f32[18,66,1]{1,2,0:T(1,128)S(1)}, u32[]{:S(2)}, u32[]{:S(2)}) collective-permute-start(f32[18,66,1]{1,2,0:T(1,128)S(1)} %copy.33), channel_id=1, source_target_pairs={{1,0},{2,1},{3,2},{5,4},{6,5},{7,6},{9,8},{10,9},{11,10},{13,12},{... | collective-permute-start | bytes 14264 | tf_op jit(solution)/shard_map/ppermute | solution.py:24
  165.7 5.7 %collective-permute-start.35 = (f32[18,66,1]{1,2,0:T(1,128)S(1)}, f32[18,66,1]{1,2,0:T(1,128)S(1)}, u32[]{:S(2)}, u32[]{:S(2)}) collective-permute-start(f32[18,66,1]{1,2,0:T(1,128)S(1)} %copy.35), channel_id=1, source_target_pairs={{0,1},{1,2},{2,3},{4,5},{5,6},{6,7},{8,9},{9,10},{10,11},{12,13},{... | collective-permute-start | bytes 14264 | tf_op jit(solution)/shard_map/ppermute | solution.py:22
  179.1 15.2 %copy-start.2 = (f32[16,64,128]{2,1,0:T(8,128)}, f32[16,64,128]{2,1,0:T(8,128)S(1)}, u32[]{:S(2)}) copy-start(f32[16,64,128]{2,1,0:T(8,128)S(1)} %get-tuple-element.292) | copy-start | bytes 1572868
  179.1 7.5 %collective-permute-start.36 = (f32[1,64,128]{2,1,0:T(8,128)S(1)}, f32[1,64,128]{2,1,0:T(8,128)S(1)}, u32[]{:S(2)}, u32[]{:S(2)}) collective-permute-start(f32[1,64,128]{2,1,0:T(8,128)S(1)} %get-tuple-element.333), channel_id=1, source_target_pairs={{16,0},{32,16},{48,32},{64,48},{80,64},{96,80},{112,96},{128,112},... | collective-permute-start | bytes 98312 | tf_op jit(solution)/shard_map/ppermute | solution.py:24
  181.0 6.6 %collective-permute-start.37 = (f32[1,64,128]{2,1,0:T(8,128)S(1)}, f32[1,64,128]{2,1,0:T(8,128)S(1)}, u32[]{:S(2)}, u32[]{:S(2)}) collective-permute-start(f32[1,64,128]{2,1,0:T(8,128)S(1)} %get-tuple-element.332), channel_id=1, source_target_pairs={{0,16},{16,32},{32,48},{48,64},{64,80},{80,96},{96,112},{112,128},... | collective-permute-start | bytes 98312 | tf_op jit(solution)/shard_map/ppermute | solution.py:22
  187.6 5.8 %collective-permute-start.38 = (f32[18,1,128]{2,1,0:T(1,128)S(1)}, f32[18,1,128]{2,1,0:T(1,128)S(1)}, u32[]{:S(2)}, u32[]{:S(2)}) collective-permute-start(f32[18,1,128]{2,1,0:T(1,128)S(1)} %get-tuple-element.319), channel_id=1, source_target_pairs={{4,0},{8,4},{12,8},{5,1},{9,5},{13,9},{6,2},{10,6},{14,10},{7,3},{... | collective-permute-start | bytes 27656 | tf_op jit(solution)/shard_map/ppermute | solution.py:24
  188.9 5.3 %collective-permute-start.39 = (f32[18,1,128]{2,1,0:T(1,128)S(1)}, f32[18,1,128]{2,1,0:T(1,128)S(1)}, u32[]{:S(2)}, u32[]{:S(2)}) collective-permute-start(f32[18,1,128]{2,1,0:T(1,128)S(1)} %get-tuple-element.318), channel_id=1, source_target_pairs={{0,4},{4,8},{8,12},{1,5},{5,9},{9,13},{2,6},{6,10},{10,14},{3,7},{... | collective-permute-start | bytes 27656 | tf_op jit(solution)/shard_map/ppermute | solution.py:22
  196.9 7.2 %collective-permute-start.40 = (f32[18,66,1]{1,2,0:T(1,128)S(1)}, f32[18,66,1]{1,2,0:T(1,128)S(1)}, u32[]{:S(2)}, u32[]{:S(2)}) collective-permute-start(f32[18,66,1]{1,2,0:T(1,128)S(1)} %copy.37), channel_id=1, source_target_pairs={{1,0},{2,1},{3,2},{5,4},{6,5},{7,6},{9,8},{10,9},{11,10},{13,12},{... | collective-permute-start | bytes 14264 | tf_op jit(solution)/shard_map/ppermute | solution.py:24
  199.6 5.7 %collective-permute-start.41 = (f32[18,66,1]{1,2,0:T(1,128)S(1)}, f32[18,66,1]{1,2,0:T(1,128)S(1)}, u32[]{:S(2)}, u32[]{:S(2)}) collective-permute-start(f32[18,66,1]{1,2,0:T(1,128)S(1)} %copy.39), channel_id=1, source_target_pairs={{0,1},{1,2},{2,3},{4,5},{5,6},{6,7},{8,9},{9,10},{10,11},{12,13},{... | collective-permute-start | bytes 14264 | tf_op jit(solution)/shard_map/ppermute | solution.py:22
  223.9 192.3 %copy-start.3 = (f32[16,64,128]{2,1,0:T(8,128)S(1)}, f32[16,64,128]{2,1,0:T(8,128)}, u32[]{:S(2)}) copy-start(f32[16,64,128]{2,1,0:T(8,128)} %get-tuple-element.301) | copy-start | bytes 1572868
  224.0 192.4 %copy-start.4 = (f32[16,64,128]{2,1,0:T(8,128)S(1)}, f32[16,64,128]{2,1,0:T(8,128)}, u32[]{:S(2)}) copy-start(f32[16,64,128]{2,1,0:T(8,128)} %get-tuple-element.299) | copy-start | bytes 1572868
  224.0 192.4 %copy-start.5 = (f32[16,64,128]{2,1,0:T(8,128)S(1)}, f32[16,64,128]{2,1,0:T(8,128)}, u32[]{:S(2)}) copy-start(f32[16,64,128]{2,1,0:T(8,128)} %get-tuple-element.297) | copy-start | bytes 1572868
  224.0 192.4 %copy-start.6 = (f32[16,64,128]{2,1,0:T(8,128)S(1)}, f32[16,64,128]{2,1,0:T(8,128)}, u32[]{:S(2)}) copy-start(f32[16,64,128]{2,1,0:T(8,128)} %get-tuple-element.295) | copy-start | bytes 1572868
  224.0 192.4 %copy-start.7 = (f32[16,64,128]{2,1,0:T(8,128)S(1)}, f32[16,64,128]{2,1,0:T(8,128)}, u32[]{:S(2)}) copy-start(f32[16,64,128]{2,1,0:T(8,128)} %get-tuple-element.293) | copy-start | bytes 1572868
  (2 other events, 30.1 us)
where the time goes:
time: 424 us; the launch traced here: 420 us
  starting transfers between devices  131 us (31%)
  blocking collectives  117 us (28%)
  local copies, waits for them, and re-layouts  58.6 us (14%)
  between operations  49.6 us (12%)
  other arithmetic  41.4 us (10%)
  matrix products  13.6 us (3%)
  waiting for transfers between devices  8.91 us (2%)
    psum x1, blocking collectives, on_device(): gram_matrix = lax.psum(local_gram, ('gx', 'gy', 'gz'))  117 us
    ppermute x21, starting transfers between devices, extended(): lax.ppermute(tail, axis, [(i, (i + 1) % count) for i in range(ends)])  89.3 us
    ppermute x21, starting transfers between devices, extended(): lax.ppermute(head, axis, [((i + 1) % count, i) for i in range(ends)])  41.8 us
    div x6, other arithmetic, next_basis(): return (image_field - basis_shift * previous) / basis_scale  33.5 us
    slice x13, local copies, waits for them, and re-layouts, extended(): head = lax.slice_in_dim(cells, 0, width, axis=dim)  13.7 us
    dot_general x1, matrix products, on_device(): local_gram = jnp.dot(stacked, stacked.T, precision=lax.Precision.HIGHEST)  12.7 us
    another operation x1, local copies, waits for them, and re-layouts, on_device(): stacked = jnp.stack(basis_list).reshape(STEPS + 1, -1)  11.1 us
    ppermute x21, waiting for transfers between devices, extended(): lax.ppermute(tail, axis, [(i, (i + 1) % count) for i in range(ends)])  8.86 us
  transfers between devices with their start and end apart: 42, of which 10 were waited for; matrix products, arithmetic and copies ran while one was open for 4% of the time, Pallas kernels for 0%

commit v1 on v0

v1 whole, which is shorter than its diff:
```python
import jax
import jax.numpy as jnp
from jax import lax
from jax.experimental import pallas as pl
from jax.experimental.pallas import tpu as pltpu
from jax.sharding import PartitionSpec as P

STEPS = 6
MOMENTS = 2 * STEPS + 1
SHIFT = 7.0
MESH = pl.DeviceIdType.MESH
F32 = jnp.float32
LANES = 128
WEIGHT = 7


def face_pair(here, other):
    liquid = other > 0.0
    total = jnp.where(liquid, here + other, 1.0)
    shared = 2.0 * here * other / total
    return jnp.where(liquid, shared, here), jnp.where(liquid, shared, 0.0)


def make_kernel(shape, counts):
    nx, ny, nz = shape
    gxn, gyn, gzn = counts
    tiles = ny // 8
    pitch = ny + 16
    halves = nx * tiles * 2 // LANES
    per_half = nx // halves
    stride = 2 * tiles
    plane = 2 * gyn * gzn
    chips = gxn // 2

    def rows_of(slab):
        return pl.ds(pl.multiple_of(slab * pitch + 8, 8), ny)

    def kernel(rs, inv, act, sol, res, rs_v, inv_v, act_v, B, YS, YG, ZS, ZG,
               HX, HY, HZM, HZP, D, MU, SA, RA, SB, RB, OS, OR,
               in_sem, out_sem, xs, xr, ys, yr, zs, zr, a_send, a_recv, b_send, b_recv):
        gx, gy, gz = lax.axis_index("gx"), lax.axis_index("gy"), lax.axis_index("gz")
        chip, core = gx // 2, gx % 2
        pos = (gx, gy, gz)

        loads = [
            pltpu.make_async_copy(src, dst, in_sem.at[i])
            for i, (src, dst) in enumerate(((rs, rs_v), (inv, inv_v), (act, act_v)))
        ]
        for copy in loads:
            copy.start()

        low = (gx > 0, gy > 0, gz > 0)
        high = (gx < gxn - 1, gy < gyn - 1, gz < gzn - 1)

        def plane_peer(d):
            t = (core + 2 * (gy + gyn * gz) + d) % plane
            return {"gx": 2 * chip + t % 2, "gy": (t // 2) % gyn, "gz": t // (2 * gyn)}

        def chip_peer(d):
            return {"gx": 2 * ((chip + d) % chips) + core}

        barrier = pltpu.get_barrier_semaphore()

        def greet(device):
            pl.semaphore_signal(barrier, inc=1, device_id=device, device_id_type=MESH)

        @pl.when((core == 0) & low[0])
        def _():
            greet({"gx": gx - 1})

        @pl.when((core == 1) & high[0])
        def _():
            greet({"gx": gx + 1})

        @pl.loop(1, plane)
        def _(d):
            greet(plane_peer(d))

        @pl.loop(1, chips)
        def _(d):
            greet(chip_peer(d))

        @pl.when(jnp.logical_not(low[0]))
        def _():
            for k in range(8):
                if k != 6:
                    B[k, pl.ds(8, ny), :] = jnp.zeros((ny, LANES), F32)

        @pl.when(jnp.logical_not(high[0]))
        def _():
            for k in range(8):
                if k != 6:
                    B[k, pl.ds((nx + 1) * pitch + 8, ny), :] = jnp.zeros((ny, LANES), F32)

        for side, there in ((0, low), (1, high)):
            @pl.when(jnp.logical_not(there[1]))
            def _():
                for k in range(8):
                    if k != 6:
                        YG[k, side] = jnp.zeros((nx, LANES), F32)

            @pl.when(jnp.logical_not(there[2]))
            def _():
                for k in range(8):
                    if k != 6:
                        ZG[k, side] = jnp.zeros((halves, 8, LANES), F32)

        for x in range(nx):
            B[WEIGHT, pl.ds((x + 1) * pitch + ny + 8, 8), :] = jnp.zeros((8, LANES), F32)

        across = ((core == 0) & low[0]) | ((core == 1) & high[0])
        pl.semaphore_wait(barrier, plane + chips - 2 + across.astype(jnp.int32))

        lane = lax.broadcasted_iota(jnp.int32, (8, LANES), 1)
        lane_s = lax.broadcasted_iota(jnp.int32, (ny, LANES), 1)
        first, last = lane_s == 0, lane_s == LANES - 1
        odd = lane % 2 == 1

        def x_copy(k, side):
            src, dst, to = ((1, nx + 1, gx - 1), (nx, 0, gx + 1))[side]
            return pltpu.make_async_remote_copy(
                B.at[k, rows_of(src)], B.at[k, rows_of(dst)], xs.at[k, side], xr.at[k, 1 - side],
                device_id={"gx": to}, device_id_type=MESH)

        def y_copy(k, side):
            return pltpu.make_async_remote_copy(
                YS.at[k, side], YG.at[k, 1 - side], ys.at[k, side], yr.at[k, 1 - side],
                device_id={"gy": gy + 2 * side - 1}, device_id_type=MESH)

        def z_copy(k, side):
            return pltpu.make_async_remote_copy(
                ZS.at[k], ZG.at[k, 1 - side], zs.at[k, side], zr.at[k, 1 - side],
                device_id={"gz": gz + 2 * side - 1}, device_id_type=MESH)

        copies = (x_copy, y_copy, z_copy)

        def on_sides(act_on, axes=(0, 1, 2)):
            for axis in axes:
                for side, there in ((0, low), (1, high)):
                    @pl.when(there[axis])
                    def _():
                        act_on(copies[axis], side)

        def y_pack(k):
            for side, row in ((0, 0), (1, ny - 1)):
                YS[k, side] = B[k, pl.ds(pitch + 8 + row, nx, stride=pitch), :]

        def y_unpack(k):
            B[k, pl.ds(pitch + 7, nx, stride=pitch), :] = YG[k, 0]
            B[k, pl.ds(pitch + 8 + ny, nx, stride=pitch), :] = YG[k, 1]

        def pack_part(slab, xi):
            ends = jnp.where(first | last, slab, 0.0)
            part = ends[0:8]
            for t in range(1, tiles):
                part = part + pltpu.roll(ends[8 * t : 8 * t + 8], 2 * t, 1)
            return pltpu.roll(part, stride * xi, 1)

        def ghost_columns(ghost, xi):
            base = pltpu.roll(ghost, (LANES - stride * xi) % LANES, 1)
            parts = [base] + [pltpu.roll(base, LANES - 2 * t, 1) for t in range(1, tiles)]
            return jnp.concatenate(parts, axis=0)

        def z_ghost(k, xo):
            return jnp.where(odd, ZG[k, 0, xo], ZG[k, 1, xo])

        def z_shift(slab, columns):
            lower = pltpu.roll(jnp.where(last, columns, slab), 1, 1)
            upper = pltpu.roll(jnp.where(first, columns, slab), LANES - 1, 1)
            return lower, upper

        def fold(slab):
            total = slab[0:8]
            for t in range(1, tiles):
                total = total + slab[8 * t : 8 * t + 8]
            return total

        for copy in loads:
            copy.wait()

        mu0 = jnp.zeros((8, LANES), F32)
        for xo in range(halves):
            def first_pass(xi, carry):
                mu, wp, bp = carry
                x = xo * per_half + xi
                liquid = act_v[x].astype(F32)
                w, b = inv_v[x] * liquid, rs_v[x] * liquid
                B[WEIGHT, rows_of(x + 1), :] = w
                B[0, rows_of(x + 1), :] = b
                return mu + fold(b * b), wp + pack_part(w, xi), bp + pack_part(b, xi)

            zero = jnp.zeros((8, LANES), F32)
            mu0, wp, bp = lax.fori_loop(0, per_half, first_pass, (mu0, zero, zero))
            ZS[WEIGHT, xo] = wp
            ZS[0, xo] = bp
        MU[0] = mu0
        y_pack(WEIGHT)
        y_pack(0)
        on_sides(lambda copy, side: copy(WEIGHT, side).start())
        on_sides(lambda copy, side: copy(0, side).start())

        on_sides(lambda copy, side: copy(WEIGHT, 1 - side).wait_recv())
        y_unpack(WEIGHT)
        scale = -1.0 / SHIFT
        for xo in range(halves):
            def face_pass(xi, _):
                x = xo * per_half + xi
                row = (x + 1) * pitch + 8
                center = B[WEIGHT, rows_of(x + 1), :]
                columns = ghost_columns(z_ghost(WEIGHT, xo), xi)
                lower, upper = z_shift(center, columns)
                total = jnp.zeros((ny, LANES), F32)
                for other, keep, at in (
                    (B[WEIGHT, rows_of(x + 2), :], HX, pl.ds(pl.multiple_of((x + 1) * ny, 8), ny)),
                    (B[WEIGHT, rows_of(x), :], HX, pl.ds(pl.multiple_of(x * ny, 8), ny)),
                    (B[WEIGHT, pl.ds(row + 1, ny), :], HY, pl.ds(row + 1, ny)),
                    (B[WEIGHT, pl.ds(row - 1, ny), :], HY, pl.ds(row, ny)),
                    (upper, HZP, pl.ds(pl.multiple_of(x * ny, 8), ny)),
                    (lower, HZM, pl.ds(pl.multiple_of(x * ny, 8), ny)),
                ):
                    face, shared = face_pair(center, other)
                    total = total + face
                    keep[at, :] = shared * scale
                D[pl.ds(pl.multiple_of(x * ny, 8), ny), :] = total * (1.0 / SHIFT) - 1.0
                return 0

            lax.fori_loop(0, per_half, face_pass, 0)

        @pl.loop(0, STEPS)
        def _(k):
            on_sides(lambda copy, side: copy(k, 1 - side).wait_recv())
            y_unpack(k)
            odd_mu = jnp.zeros((8, LANES), F32)
            even_mu = jnp.zeros((8, LANES), F32)
            for xo in range(halves):
                ghost = z_ghost(k, xo)

                def step(xi, carry):
                    mixed, square, packed = carry
                    x = xo * per_half + xi
                    row = (x + 1) * pitch + 8
                    flat = pl.ds(pl.multiple_of(x * ny, 8), ny)
                    above = pl.ds(pl.multiple_of((x + 1) * ny, 8), ny)
                    center = B[k, rows_of(x + 1), :]
                    lower, upper = z_shift(center, ghost_columns(ghost, xi))
                    image = D[flat, :] * center
                    image = image + HX[above, :] * B[k, rows_of(x + 2), :]
                    image = image + HX[flat, :] * B[k, rows_of(x), :]
                    image = image + HY[pl.ds(row + 1, ny), :] * B[k, pl.ds(row + 1, ny), :]
                    image = image + HY[pl.ds(row, ny), :] * B[k, pl.ds(row - 1, ny), :]
                    image = image + HZP[flat, :] * upper
                    image = image + HZM[flat, :] * lower
                    B[k + 1, rows_of(x + 1), :] = image
                    return (mixed + fold(center * image), square + fold(image * image),
                            packed + pack_part(image, xi))

                odd_mu, even_mu, packed = lax.fori_loop(
                    0, per_half, step, (odd_mu, even_mu, jnp.zeros((8, LANES), F32)))
                ZS[k + 1, xo] = packed
            MU[2 * k + 1] = odd_mu
            MU[2 * k + 2] = even_mu

            @pl.when(k < STEPS - 1)
            def _():
                y_pack(k + 1)
                on_sides(lambda copy, side: copy(k + 1, side).start())

        for spare in range(MOMENTS, 16):
            MU[spare] = jnp.zeros((8, LANES), F32)
        local = jnp.sum(jnp.sum(MU[...], axis=1), axis=1, keepdims=True)
        diagonal = (lax.broadcasted_iota(jnp.int32, (16, LANES), 0)
                    == lax.broadcasted_iota(jnp.int32, (16, LANES), 1))
        row = jnp.sum(jnp.where(diagonal, jnp.broadcast_to(local, (16, LANES)), 0.0), axis=0, keepdims=True)

        def all_sum(row, staged, landed, send, recv, peers, me, peer):
            staged[...] = row
            landed[me] = row

            @pl.loop(1, peers)
            def _(d):
                pltpu.make_async_remote_copy(
                    staged, landed.at[me], send, recv, device_id=peer(d), device_id_type=MESH).start()

            whole = landed.at[pl.ds(0, peers - 1)]
            pltpu.make_async_copy(whole, whole, recv).wait()
            total = landed[0]
            for i in range(1, peers):
                total = total + landed[i]
            return total

        row = all_sum(row, SA, RA, a_send, a_recv, plane, core + 2 * (gy + gyn * gz), plane_peer)
        row = all_sum(row, SB, RB, b_send, b_recv, chips, chip, chip_peer)

        spread = jnp.broadcast_to(row, (8, LANES))
        mu = [jnp.broadcast_to(spread[:, i : i + 1], (8, LANES)) for i in range(MOMENTS)]
        size = STEPS + 1
        gram = [[mu[i + j] for j in range(size)] for i in range(size)]
        side = [jnp.full((8, LANES), (-1.0) ** i, F32) for i in range(size)]
        inverse = []
        for p in range(size):
            inverse.append(1.0 / gram[p][p])
            for i in range(p + 1, size):
                factor = gram[p][i] * inverse[p]
                for j in range(i, size):
                    gram[i][j] = gram[i][j] - factor * gram[p][j]
                side[i] = side[i] - factor * side[p]
        solved = [None] * size
        for i in reversed(range(size)):
            running = side[i]
            for j in range(i + 1, size):
                running = running - gram[i][j] * solved[j]
            solved[i] = running * inverse[i]
        norm = solved[0]
        for i in range(1, size):
            norm = norm - solved[i] if i % 2 else norm + solved[i]
        norm = 1.0 / norm
        leftover = [value * norm for value in solved]
        scaled = [None] * STEPS
        scaled[STEPS - 1] = -leftover[STEPS]
        for i in reversed(range(STEPS - 1)):
            scaled[i] = -leftover[i + 1] - scaled[i + 1]
        for i in range(STEPS):
            MU[i] = scaled[i] * (1.0 / SHIFT)
        for i in range(size):
            MU[8 + i] = leftover[i]

        chunk = 4

        def out_copies(part):
            at = pl.ds(part * chunk, chunk)
            return [pltpu.make_async_copy(src.at[at], dst.at[at], out_sem.at[i, part])
                    for i, (src, dst) in enumerate(((OS, sol), (OR, res)))]

        @pl.loop(0, nx // chunk)
        def _(part):
            @pl.loop(0, chunk)
            def _(within):
                x = part * chunk + within
                for t in range(tiles):
                    at = pl.ds(pl.multiple_of((x + 1) * pitch + 8 + 8 * t, 8), 8)
                    value = B[0, at, :]
                    s, r = MU[0] * value, MU[8] * value
                    for i in range(1, size):
                        value = B[i, at, :]
                        if i < STEPS:
                            s = s + MU[i] * value
                        r = r + MU[8 + i] * value
                    OS[x, pl.ds(8 * t, 8), :] = s
                    OR[x, pl.ds(8 * t, 8), :] = r

            for copy in out_copies(part):
                copy.start()

        for k in tuple(range(STEPS)) + (WEIGHT,):
            on_sides(lambda copy, side: copy(k, side).wait_send())
        for landed, send, peers in ((RA, a_send, plane), (RB, b_send, chips)):
            whole = landed.at[pl.ds(0, peers - 1)]
            pltpu.make_async_copy(whole, whole, send).wait()

        @pl.loop(0, nx // chunk)
        def _(part):
            for copy in out_copies(part):
                copy.wait()

    scratch = [
        pltpu.VMEM((nx, ny, nz), F32), pltpu.VMEM((nx, ny, nz), F32), pltpu.VMEM((nx, ny, nz), jnp.int32),
        pltpu.VMEM((8, (nx + 2) * pitch, LANES), F32),
        pltpu.VMEM((8, 2, nx, LANES), F32), pltpu.VMEM((8, 2, nx, LANES), F32),
        pltpu.VMEM((8, halves, 8, LANES), F32), pltpu.VMEM((8, 2, halves, 8, LANES), F32),
        pltpu.VMEM(((nx + 1) * ny, LANES), F32), pltpu.VMEM(((nx + 2) * pitch, LANES), F32),
        pltpu.VMEM((nx * ny, LANES), F32), pltpu.VMEM((nx * ny, LANES), F32),
        pltpu.VMEM((nx * ny, LANES), F32),
        pltpu.VMEM((16, 8, LANES), F32),
        pltpu.VMEM((1, LANES), F32), pltpu.VMEM((plane, 1, LANES), F32),
        pltpu.VMEM((1, LANES), F32), pltpu.VMEM((chips, 1, LANES), F32),
        pltpu.VMEM((nx, ny, nz), F32), pltpu.VMEM((nx, ny, nz), F32),
        pltpu.SemaphoreType.DMA((3,)), pltpu.SemaphoreType.DMA((2, 4)),
    ] + [pltpu.SemaphoreType.DMA((8, 2))] * 6 + [pltpu.SemaphoreType.DMA] * 4
    return kernel, scratch


def solution(mesh):
    counts = tuple(mesh.shape[axis] for axis in ("gx", "gy", "gz"))

    def on_device(right_side, inv_density, active):
        kernel, scratch = make_kernel(right_side.shape, counts)
        field = jax.ShapeDtypeStruct(right_side.shape, F32)
        return pl.pallas_call(
            kernel,
            out_shape=(field, field),
            in_specs=[pl.BlockSpec(memory_space=pl.ANY)] * 3,
            out_specs=(pl.BlockSpec(memory_space=pl.ANY),) * 2,
            scratch_shapes=scratch,
            compiler_params=pltpu.CompilerParams(collective_id=0, has_side_effects=True),
        )(right_side, inv_density, active)

    placed = P("gx", "gy", "gz")
    return jax.shard_map(
        on_device, mesh=mesh, in_specs=(placed,) * 3, out_specs=(placed,) * 2, check_vma=False)
```

time: 424 us -> 94.3 us (0.22)
  starting transfers between devices: 131 us -> 0 us
  blocking collectives: 117 us -> 0 us
  Pallas kernels: 0 us -> 90.8 us
  local copies, waits for them, and re-layouts: 58.6 us -> 2.74 us
  between operations: 49.6 us -> 0.65 us
  other arithmetic: 41.4 us -> 0 us
  matrix products: 13.6 us -> 0 us
  waiting for transfers between devices: 8.91 us -> 0 us
    ppermute x42 -> x0, starting transfers between devices: 131 us -> none  [the longest x21 89.3 us: extended(): lax.ppermute(tail, axis, [(i, (i + 1) % count) for i in range(ends)])]
    psum x1 -> x0, blocking collectives: 117 us -> none  [on_device(): gram_matrix = lax.psum(local_gram, ('gx', 'gy', 'gz'))]
    pallas_call x0 -> x1, Pallas kernels: none -> 90.8 us  [on_device(): pl.pallas_call(kernel, out_shape=(field, field), in_specs=[pl.BlockSpec(m...]
    div x7 -> x0, other arithmetic: 33.5 us -> none  [the longest x6 33.5 us: next_basis(): return (image_field - basis_shift * previous) / basis_scale]
    slice x46 -> x0, local copies, waits for them, and re-layouts: 31.4 us -> none  [the longest x13 13.7 us: extended(): head = lax.slice_in_dim(cells, 0, width, axis=dim)]
    ppermute x14 -> x0, local copies, waits for them, and re-layouts: 15.7 us -> none  [the longest x7 8.41 us: extended(): lax.ppermute(tail, axis, [(i, (i + 1) % count) for i in range(ends)])]
    dot_general x3 -> x0, matrix products: 13.6 us -> none  [the longest x1 12.7 us: on_device(): local_gram = jnp.dot(stacked, stacked.T, precision=lax.Precision.HIGHEST)]
    another operation x2 -> x0, local copies, waits for them, and re-layouts: 11.2 us -> none  [the longest x1 11.1 us: on_device(): stacked = jnp.stack(basis_list).reshape(STEPS + 1, -1)]
  transfers between devices with their start and end apart: 42 -> 0, of which waited for: 10 -> 0; matrix products, arithmetic and copies ran while one was open for 4% -> 0% of each run, Pallas kernels for 0% -> 0%
where the time goes in v1:
time: 94.3 us; the launch traced here: 94.2 us
  Pallas kernels  90.8 us (96%)
  local copies, waits for them, and re-layouts  2.74 us (3%)
    pallas_call x1, Pallas kernels, on_device(): pl.pallas_call(kernel, out_shape=(field, field), in_specs=[pl.BlockSpec(m...  90.8 us
    unnamed x4, local copies, waits for them, and re-layouts  2.74 us

profile of v1, /device:TPU:1, one launch (start us, length us, event | category | flops | bytes accessed | tf_op | source)
XLA Modules:
  0.0 94.2 jit_solution(11503620657089709432)
XLA Ops:
  0.6 90.8 %shard_map.50 = (f32[16,64,128]{2,1,0:T(8,128)}, f32[16,64,128]{2,1,0:T(8,128)}) custom-call(f32[16,64,128]{2,1,0:T(8,128)} %rs.1, f32[16,64,128]{2,1,0:T(8,128)} %inv.1, s32[16,64,128]{2,1,0:T(8,128)} %act.1), custom_call_target="tpu_custom_call" | custom-call | tf_op jit(solution)/shard_map/pallas_call | solution.py:388
  91.5 0.0 copy-start
  91.5 1.9 %copy.7 = f32[16,64,128]{2,1,0:T(8,128)} copy(f32[16,64,128]{2,1,0:T(8,128)} %get-tuple-element.4) | data formatting | bytes 1048576
  93.4 0.0 copy-done
  93.4 0.8 copy.8
Async XLA Ops:
  91.5 2.0 %copy-start = (f32[16,64,128]{2,1,0:T(8,128)S(1)}, f32[16,64,128]{2,1,0:T(8,128)}, u32[]{:S(2)}) copy-start(f32[16,64,128]{2,1,0:T(8,128)} %get-tuple-element.5) | copy-start | bytes 1572868

commit v2 on v1

v2 whole, which is shorter than its diff:
```python
import jax
import jax.numpy as jnp
from jax import lax
from jax.experimental import pallas as pl
from jax.experimental.pallas import tpu as pltpu
from jax.sharding import PartitionSpec as P

STEPS = 6
SIZE = STEPS + 1
MOMENTS = 2 * STEPS + 1
SHIFT = 7.0
MESH = pl.DeviceIdType.MESH
F32 = jnp.float32
LANES = 128
WEIGHT = 7
SLOTS = tuple(range(STEPS)) + (WEIGHT,)


def scaled_face(here, other):
    total = jnp.where(other > 0.0, here + other, 1.0)
    return (here * (-2.0 / SHIFT)) * other / total


def tree(values):
    values = list(values)
    while len(values) > 1:
        values = [values[i] + values[i + 1] if i + 1 < len(values) else values[i]
                  for i in range(0, len(values), 2)]
    return values[0]


class Sums:
    def __init__(self, count=4):
        self.parts, self.turn = [None] * count, 0

    def add(self, value):
        held = self.parts[self.turn]
        self.parts[self.turn] = value if held is None else held + value
        self.turn = (self.turn + 1) % len(self.parts)

    def total(self):
        return tree([part for part in self.parts if part is not None])


def make_kernel(shape, counts):
    nx, ny, nz = shape
    gxn, gyn, gzn = counts
    tiles = ny // 8
    pitch = ny + 16
    halves = nx * tiles * 2 // LANES
    plane = 2 * gyn * gzn
    chips = gxn // 2
    chunk = 4

    def row(x, t=0):
        return (x + 1) * pitch + 8 + 8 * t

    def at(x, t):
        return pl.ds(row(x, t), 8)

    def flat(x, t):
        return pl.ds(x * ny + 8 * t, 8)

    def slab(x):
        return pl.ds(row(x), ny)

    def place(x, t):
        j = x * tiles + t
        return j // (LANES // 2), 2 * (j % (LANES // 2))

    def turn(value, amount):
        amount %= LANES
        return pltpu.roll(value, amount, 1) if amount else value

    def is_rim(x, t):
        return x in (0, nx - 1) or t in (0, tiles - 1)

    every = [(x, t) for x in range(nx) for t in range(tiles)]
    inner = [xt for xt in every if not is_rim(*xt)]
    caps = [xt for xt in every if xt[0] in (0, nx - 1)]
    sides_y = [xt for xt in every if is_rim(*xt) and xt[0] not in (0, nx - 1)]

    def kernel(rs, inv, act, sol, res, rs_v, inv_v, act_v, B, YS, YG, ZS, ZG,
               HX, HY, HYG, HZM, HZP, FP, D, MU, SA, RA, SB, RB, OS, OR,
               in_sem, out_sem, xs, xr, ys, yr, zs, zr, a_send, a_recv, b_send, b_recv, far):
        gx, gy, gz = lax.axis_index("gx"), lax.axis_index("gy"), lax.axis_index("gz")
        chip, core = gx // 2, gx % 2
        nil = gx // 4096

        def near(start):
            return pl.ds(nil + start, 8)

        def load_copies(part):
            where = pl.ds(part * chunk, chunk)
            return [pltpu.make_async_copy(src.at[where], dst.at[where], in_sem.at[i, part])
                    for i, (src, dst) in enumerate(((rs, rs_v), (inv, inv_v), (act, act_v)))]

        for part in range(nx // chunk):
            for copy in load_copies(part):
                copy.start()

        low = (gx > 0, gy > 0, gz > 0)
        high = (gx < gxn - 1, gy < gyn - 1, gz < gzn - 1)
        names = ("gx", "gy", "gz")
        pos = (gx, gy, gz)

        def chip_peer(d):
            return {"gx": (gx + 2 * d) % gxn}

        barrier = pltpu.get_barrier_semaphore()

        def greet(semaphore, device):
            pl.semaphore_signal(semaphore, inc=1, device_id=device, device_id_type=MESH)

        present = 2
        for axis in range(3):
            for there, step in ((low, -1), (high, 1)):
                present = present + there[axis].astype(jnp.int32)

                @pl.when(there[axis])
                def _():
                    greet(barrier, {names[axis]: pos[axis] + step})

        greet(barrier, chip_peer(1))
        greet(barrier, chip_peer(chips - 1))

        for side, there in ((0, low), (1, high)):
            @pl.when(jnp.logical_not(there[0]))
            def _():
                for k in SLOTS:
                    B[k, slab((-1, nx)[side]), :] = jnp.zeros((ny, LANES), F32)

            @pl.when(jnp.logical_not(there[1]))
            def _():
                for k in SLOTS:
                    YG[k, side] = jnp.zeros((nx, LANES), F32)

            @pl.when(jnp.logical_not(there[2]))
            def _():
                for k in SLOTS:
                    ZG[k, side] = jnp.zeros((halves, 8, LANES), F32)

        none = jnp.zeros((nx, LANES), F32)
        for k in SLOTS:
            B[k, pl.ds(row(0) - 1, nx, stride=pitch), :] = none
            B[k, pl.ds(row(0) + ny, nx, stride=pitch), :] = none
        HY[pl.ds(row(0) + ny, nx, stride=pitch), :] = none
        for spare in (0, 14, 15):
            MU[spare] = jnp.zeros((8, LANES), F32)

        lane = lax.broadcasted_iota(jnp.int32, (8, LANES), 1)
        first, last = lane == 0, lane == LANES - 1
        ends = first | last
        odd = lane % 2 == 1

        def x_copy(k, side):
            src, dst = ((0, nx), (nx - 1, -1))[side]
            return pltpu.make_async_remote_copy(
                B.at[k, slab(src)], B.at[k, slab(dst)], xs.at[k, side], xr.at[k, 1 - side],
                device_id={"gx": gx + 2 * side - 1}, device_id_type=MESH)

        def y_copy(k, side):
            return pltpu.make_async_remote_copy(
                YS.at[k, side], YG.at[k, 1 - side], ys.at[k, side], yr.at[k, 1 - side],
                device_id={"gy": gy + 2 * side - 1}, device_id_type=MESH)

        def z_copy(k, side):
            return pltpu.make_async_remote_copy(
                ZS.at[k], ZG.at[k, 1 - side], zs.at[k, side], zr.at[k, 1 - side],
                device_id={"gz": gz + 2 * side - 1}, device_id_type=MESH)

        copies = (x_copy, y_copy, z_copy)

        def on_sides(axes, act_on):
            for axis in axes:
                for side, there in ((0, low), (1, high)):
                    @pl.when(there[axis])
                    def _():
                        act_on(copies[axis], side)

        def send(k, axes):
            on_sides(axes, lambda copy, side: copy(k, side).start())

        def arrive(k, axes=(0, 1, 2)):
            on_sides(axes, lambda copy, side: copy(k, 1 - side).wait_recv())

        y_rows = tuple(pl.ds(row(0) + y, nx, stride=pitch) for y in (0, ny - 1))

        def y_pack(k):
            for side in range(2):
                YS[k, side] = B[k, y_rows[side], :]

        def packed(value, x, t):
            return turn(jnp.where(ends, value, 0.0), place(x, t)[1])

        def unpacked(value, x, t):
            half, amount = place(x, t)
            return jnp.where(ends, turn(value[half], -amount), 0.0)

        def z_ghost(k):
            return [jnp.where(odd, turn(ZG[k, 1, half], -1), turn(ZG[k, 0, half], 1))
                    for half in range(halves)]

        for part in range(nx // chunk):
            for copy in load_copies(part):
                copy.wait()
            sums = {}
            for x in range(part * chunk, (part + 1) * chunk):
                for t in range(tiles):
                    rows = pl.ds(8 * t, 8)
                    liquid = act_v[x, rows, :].astype(F32)
                    w, b = inv_v[x, rows, :] * liquid, rs_v[x, rows, :] * liquid
                    B[WEIGHT, at(x, t), :] = w
                    B[0, at(x, t), :] = b
                    half = place(x, t)[0]
                    for k, value in ((WEIGHT, w), (0, b)):
                        sums.setdefault((k, half), Sums()).add(packed(value, x, t))
            for (k, half), total in sums.items():
                begins = place(part * chunk, 0)[1] == 0
                ZS[k, half] = total.total() if begins else ZS[k, half] + total.total()
        y_pack(WEIGHT)
        y_pack(0)
        pl.semaphore_wait(barrier, present)
        send(WEIGHT, (0, 1, 2))
        send(0, (0, 1, 2))
        greet(far.at[0], chip_peer(1))
        greet(far.at[0], chip_peer(chips - 1))

        for x in range(nx):
            for t in range(tiles):
                w = B[WEIGHT, at(x, t), :]
                if x < nx - 1:
                    HX[flat(x + 1, t), :] = scaled_face(w, B[WEIGHT, at(x + 1, t), :])
                HY[at(x, t), :] = scaled_face(w, B[WEIGHT, near(row(x, t) - 1), :])
                upper = scaled_face(w, jnp.where(last, 0.0, turn(w, -1)))
                HZP[flat(x, t), :] = upper
                HZM[flat(x, t), :] = jnp.where(first, 0.0, turn(upper, 1))
            for t in range(tiles):
                w = B[WEIGHT, at(x, t), :]
                dry = w * (-1.0 / SHIFT)
                terms = []
                for inside, other, face in (
                    (x < nx - 1, lambda: B[WEIGHT, at(x + 1, t), :], lambda: HX[flat(x + 1, t), :]),
                    (x > 0, lambda: B[WEIGHT, at(x - 1, t), :], lambda: HX[flat(x, t), :]),
                    (True, lambda: B[WEIGHT, near(row(x, t) + 1), :], lambda: HY[near(row(x, t) + 1), :]),
                    (True, lambda: B[WEIGHT, near(row(x, t) - 1), :], lambda: HY[at(x, t), :]),
                    (True, lambda: jnp.where(last, 0.0, turn(w, -1)), lambda: HZP[flat(x, t), :]),
                    (True, lambda: jnp.where(first, 0.0, turn(w, 1)), lambda: HZM[flat(x, t), :]),
                ):
                    terms.append(jnp.where(other() > 0.0, face(), dry) if inside else dry)
                D[flat(x, t), :] = -1.0 - tree(terms)

        arrive(WEIGHT)

        def ghost_face(here, other):
            face = scaled_face(here, other)
            return face, jnp.where(other > 0.0, here * (-1.0 / SHIFT) - face, 0.0)

        for side, x, there in ((0, 0, -1), (1, nx - 1, nx)):
            for t in range(tiles):
                face, change = ghost_face(B[WEIGHT, at(x, t), :], B[WEIGHT, at(there, t), :])
                HX[flat((0, nx)[side], t), :] = face
                D[flat(x, t), :] = D[flat(x, t), :] + change
        for side in range(2):
            face, change = ghost_face(B[WEIGHT, y_rows[side], :], YG[WEIGHT, side])
            HYG[side] = face
            rows = pl.ds((0, ny - 1)[side], nx, stride=ny)
            D[rows, :] = D[rows, :] + change
        ghosts = z_ghost(WEIGHT)
        changes = []
        for half in range(halves):
            face, change = ghost_face(ZS[WEIGHT, half], ghosts[half])
            FP[half] = face
            changes.append(change)
        for x, t in every:
            D[flat(x, t), :] = D[flat(x, t), :] + unpacked(changes, x, t)

        def moments(k, before):
            mixed, square = Sums(), Sums()
            for x, t in every:
                value = B[k, at(x, t), :]
                mixed.add(value * B[before, at(x, t), :])
                square.add(value * value)
            MU[2 * k] = mixed.total()
            MU[2 * k + 1] = square.total()

        @pl.loop(0, STEPS)
        def _(k):
            before = jnp.maximum(k - 1, 0)
            mixed, square = Sums(), Sums()
            ahead = [Sums() for _ in range(halves)]
            for x, t in every:
                center = B[k, at(x, t), :]
                terms = [D[flat(x, t), :] * center]
                if x < nx - 1:
                    terms.append(HX[flat(x + 1, t), :] * B[k, at(x + 1, t), :])
                if x > 0:
                    terms.append(HX[flat(x, t), :] * B[k, at(x - 1, t), :])
                terms.append(HY[near(row(x, t) + 1), :] * B[k, near(row(x, t) + 1), :])
                terms.append(HY[at(x, t), :] * B[k, near(row(x, t) - 1), :])
                terms.append(HZP[flat(x, t), :] * turn(center, -1))
                terms.append(HZM[flat(x, t), :] * turn(center, 1))
                image = tree(terms)
                B[k + 1, at(x, t), :] = image
                mixed.add(center * B[before, at(x, t), :])
                square.add(center * center)
                if not is_rim(x, t):
                    ahead[place(x, t)[0]].add(packed(image, x, t))
            MU[2 * k] = mixed.total()
            MU[2 * k + 1] = square.total()
            for half in range(halves):
                ZS[k + 1, half] = ahead[half].total()

            for when, round_id in ((1, 0), (3, 1)):
                @pl.when(k == when)
                def _():
                    pl.semaphore_wait(far.at[round_id], 2)
                    greet(far.at[round_id + 1], chip_peer(2 << round_id))
                    greet(far.at[round_id + 1], chip_peer(chips - (2 << round_id)))

            arrive(k)
            for side in range(2):
                B[k + 1, y_rows[side], :] = B[k + 1, y_rows[side], :] + HYG[side] * YG[k, side]
            ghosts = z_ghost(k)
            extra = [FP[half] * ghosts[half] for half in range(halves)]
            rim = [Sums() for _ in range(halves)]
            for x, t in caps:
                face, there = (0, -1) if x == 0 else (nx, nx)
                value = B[k + 1, at(x, t), :] + HX[flat(face, t), :] * B[k, at(there, t), :]
                rim[place(x, t)[0]].add(packed(value, x, t))
                B[k + 1, at(x, t), :] = value + unpacked(extra, x, t)

            @pl.when(k < STEPS - 1)
            def _():
                send(k + 1, (0,))

            for x, t in sides_y:
                value = B[k + 1, at(x, t), :]
                rim[place(x, t)[0]].add(packed(value, x, t))
                B[k + 1, at(x, t), :] = value + unpacked(extra, x, t)
            for half in range(halves):
                ZS[k + 1, half] = ZS[k + 1, half] + (rim[half].total() + extra[half])

            @pl.when(k < STEPS - 1)
            def _():
                y_pack(k + 1)
                send(k + 1, (2, 1))

            for x, t in inner:
                B[k + 1, at(x, t), :] = B[k + 1, at(x, t), :] + unpacked(extra, x, t)

        moments(STEPS, STEPS - 1)

        local = jnp.sum(jnp.sum(MU[...], axis=1), axis=1, keepdims=True)
        diagonal = (lax.broadcasted_iota(jnp.int32, (16, LANES), 0)
                    == lax.broadcasted_iota(jnp.int32, (16, LANES), 1))
        line = jnp.sum(jnp.where(diagonal, jnp.broadcast_to(local, (16, LANES)), 0.0), axis=0, keepdims=True)

        def all_sum(line, staged, landed, sent, got, me, peers, meanwhile):
            staged[...] = line
            landed[me] = line
            for peer in peers:
                pltpu.make_async_remote_copy(
                    staged, landed.at[me], sent, got, device_id=peer, device_id_type=MESH).start()
            meanwhile()
            others = landed.at[pl.ds(0, len(peers))]
            pltpu.make_async_copy(others, others, got).wait()
            return tree([landed[i] for i in range(len(peers) + 1)])

        def drain_halos():
            for k in SLOTS:
                on_sides((0, 1, 2), lambda copy, side: copy(k, side).wait_send())

        def far_known():
            pl.semaphore_wait(far.at[2], 2)

        plane_peers = []
        for c in range(2):
            for dy in range(gyn):
                for dz in range(gzn):
                    if c or dy or dz:
                        plane_peers.append({
                            "gx": gx + 1 - 2 * core if c else gx,
                            "gy": (gy + dy) % gyn, "gz": (gz + dz) % gzn})
        line = all_sum(line, SA, RA, a_send, a_recv, core + 2 * (gy + gyn * gz), plane_peers, far_known)
        line = all_sum(line, SB, RB, b_send, b_recv, chip, [chip_peer(d) for d in range(1, chips)], drain_halos)

        spread = jnp.broadcast_to(line, (8, LANES))
        mu = [jnp.broadcast_to(spread[:, i + 1 : i + 2], (8, LANES)) for i in range(MOMENTS)]
        gram = [[mu[i + j] for j in range(SIZE)] for i in range(SIZE)]
        right = [jnp.full((8, LANES), (-1.0) ** i, F32) for i in range(SIZE)]
        inverse = []
        for p in range(SIZE):
            inverse.append(1.0 / gram[p][p])
            for i in range(p + 1, SIZE):
                factor = gram[p][i] * inverse[p]
                for j in range(i, SIZE):
                    gram[i][j] = gram[i][j] - factor * gram[p][j]
                right[i] = right[i] - factor * right[p]
        solved = [None] * SIZE
        for i in reversed(range(SIZE)):
            running = right[i]
            for j in reversed(range(i + 1, SIZE)):
                running = running - gram[i][j] * solved[j]
            solved[i] = running * inverse[i]
        norm = 1.0 / tree([value if i % 2 == 0 else -value for i, value in enumerate(solved)])
        leftover = [value * norm for value in solved]
        scaled = [None] * STEPS
        scaled[STEPS - 1] = -leftover[STEPS]
        for i in reversed(range(STEPS - 1)):
            scaled[i] = -leftover[i + 1] - scaled[i + 1]
        weights = [value * (1.0 / SHIFT) for value in scaled]

        def out_copies(part):
            where = pl.ds(part * chunk, chunk)
            return [pltpu.make_async_copy(src.at[where], dst.at[where], out_sem.at[i, part])
                    for i, (src, dst) in enumerate(((OS, sol), (OR, res)))]

        @pl.loop(0, nx // chunk)
        def _(part):
            for within in range(chunk):
                x = part * chunk + within
                for t in range(tiles):
                    where = pl.ds(pl.multiple_of((x + 1) * pitch + 8 + 8 * t, 8), 8)
                    values = [B[i, where, :] for i in range(SIZE)]
                    OS[x, pl.ds(8 * t, 8), :] = tree([weights[i] * values[i] for i in range(STEPS)])
                    OR[x, pl.ds(8 * t, 8), :] = tree([leftover[i] * values[i] for i in range(SIZE)])

            for copy in out_copies(part):
                copy.start()

        for landed, sent, count in ((RA, a_send, plane), (RB, b_send, chips)):
            others = landed.at[pl.ds(0, count - 1)]
            pltpu.make_async_copy(others, others, sent).wait()

        @pl.loop(0, nx // chunk)
        def _(part):
            for copy in out_copies(part):
                copy.wait()

    scratch = [
        pltpu.VMEM((nx, ny, nz), F32), pltpu.VMEM((nx, ny, nz), F32), pltpu.VMEM((nx, ny, nz), jnp.int32),
        pltpu.VMEM((8, (nx + 2) * pitch, LANES), F32),
        pltpu.VMEM((8, 2, nx, LANES), F32), pltpu.VMEM((8, 2, nx, LANES), F32),
        pltpu.VMEM((8, halves, 8, LANES), F32), pltpu.VMEM((8, 2, halves, 8, LANES), F32),
        pltpu.VMEM(((nx + 1) * ny, LANES), F32), pltpu.VMEM(((nx + 2) * pitch, LANES), F32),
        pltpu.VMEM((2, nx, LANES), F32),
        pltpu.VMEM((nx * ny, LANES), F32), pltpu.VMEM((nx * ny, LANES), F32),
        pltpu.VMEM((halves, 8, LANES), F32),
        pltpu.VMEM((nx * ny, LANES), F32),
        pltpu.VMEM((16, 8, LANES), F32),
        pltpu.VMEM((1, LANES), F32), pltpu.VMEM((plane, 1, LANES), F32),
        pltpu.VMEM((1, LANES), F32), pltpu.VMEM((chips, 1, LANES), F32),
        pltpu.VMEM((nx, ny, nz), F32), pltpu.VMEM((nx, ny, nz), F32),
        pltpu.SemaphoreType.DMA((3, nx // chunk)), pltpu.SemaphoreType.DMA((2, nx // chunk)),
    ] + [pltpu.SemaphoreType.DMA((8, 2))] * 6 + [pltpu.SemaphoreType.DMA] * 4 + [
        pltpu.SemaphoreType.REGULAR((3,))]
    return kernel, scratch


def solution(mesh):
    counts = tuple(mesh.shape[axis] for axis in ("gx", "gy", "gz"))

    def on_device(right_side, inv_density, active):
        kernel, scratch = make_kernel(right_side.shape, counts)
        field = jax.ShapeDtypeStruct(right_side.shape, F32)
        return pl.pallas_call(
            kernel,
            out_shape=(field, field),
            in_specs=[pl.BlockSpec(memory_space=pl.ANY)] * 3,
            out_specs=(pl.BlockSpec(memory_space=pl.ANY),) * 2,
            scratch_shapes=scratch,
            compiler_params=pltpu.CompilerParams(collective_id=0, has_side_effects=True),
        )(right_side, inv_density, active)

    placed = P("gx", "gy", "gz")
    return jax.shard_map(
        on_device, mesh=mesh, in_specs=(placed,) * 3, out_specs=(placed,) * 2, check_vma=False)
```

time: 94.3 us -> 52.1 us (0.55)
  Pallas kernels: 90.8 us -> 48.6 us
    pallas_call x1, Pallas kernels: 90.8 us -> 48.6 us  [on_device(): pl.pallas_call(kernel, out_shape=(field, field), in_specs=[pl.BlockSpec(m...]
where the time goes in v2:
time: 52.1 us; the launch traced here: 52 us
  Pallas kernels  48.6 us (93%)
  local copies, waits for them, and re-layouts  2.74 us (5%)
  between operations  0.65 us (1%)
    pallas_call x1, Pallas kernels, on_device(): pl.pallas_call(kernel, out_shape=(field, field), in_specs=[pl.BlockSpec(m...  48.6 us
    unnamed x4, local copies, waits for them, and re-layouts  2.74 us

profile of v2, /device:TPU:1, one launch (start us, length us, event | category | flops | bytes accessed | tf_op | source)
XLA Modules:
  0.0 52.0 jit_solution(15813881254819998475)
XLA Ops:
  0.6 48.6 %shard_map.50 = (f32[16,64,128]{2,1,0:T(8,128)}, f32[16,64,128]{2,1,0:T(8,128)}) custom-call(f32[16,64,128]{2,1,0:T(8,128)} %rs.1, f32[16,64,128]{2,1,0:T(8,128)} %inv.1, s32[16,64,128]{2,1,0:T(8,128)} %act.1), custom_call_target="tpu_custom_call" | custom-call | tf_op jit(solution)/shard_map/pallas_call | solution.py:467
  49.2 0.0 copy-start
  49.2 1.9 %copy.7 = f32[16,64,128]{2,1,0:T(8,128)} copy(f32[16,64,128]{2,1,0:T(8,128)} %get-tuple-element.4) | data formatting | bytes 1048576
  51.2 0.0 copy-done
  51.2 0.8 %copy.8 = f32[16,64,128]{2,1,0:T(8,128)} copy(f32[16,64,128]{2,1,0:T(8,128)S(1)} %copy-done) | data formatting | bytes 1048576
Async XLA Ops:
  49.2 2.0 %copy-start = (f32[16,64,128]{2,1,0:T(8,128)S(1)}, f32[16,64,128]{2,1,0:T(8,128)}, u32[]{:S(2)}) copy-start(f32[16,64,128]{2,1,0:T(8,128)} %get-tuple-element.5) | copy-start | bytes 1572868

commit v3 on v2

--- a/solution.py
+++ b/solution.py
@@ -80,9 +80,9 @@
     caps = [xt for xt in every if xt[0] in (0, nx - 1)]
     sides_y = [xt for xt in every if is_rim(*xt) and xt[0] not in (0, nx - 1)]
 
-    def kernel(rs, inv, act, sol, res, rs_v, inv_v, act_v, B, YS, YG, ZS, ZG,
-               HX, HY, HYG, HZM, HZP, FP, D, MU, SA, RA, SB, RB, OS, OR,
-               in_sem, out_sem, xs, xr, ys, yr, zs, zr, a_send, a_recv, b_send, b_recv, far):
+    def kernel(rs, inv, act, B, FACTORS, rs_v, inv_v, act_v, YS, YG, ZS, ZG,
+               HX, HY, HYG, HZM, HZP, FP, CP, D, LS, SA, RA, SB, RB,
+               in_sem, xs, xr, ys, yr, zs, zr, a_send, a_recv, b_send, b_recv, far):
         gx, gy, gz = lax.axis_index("gx"), lax.axis_index("gy"), lax.axis_index("gz")
         chip, core = gx // 2, gx % 2
         nil = gx // 4096
@@ -145,8 +145,7 @@
             B[k, pl.ds(row(0) - 1, nx, stride=pitch), :] = none
             B[k, pl.ds(row(0) + ny, nx, stride=pitch), :] = none
         HY[pl.ds(row(0) + ny, nx, stride=pitch), :] = none
-        for spare in (0, 14, 15):
-            MU[spare] = jnp.zeros((8, LANES), F32)
+        LS[...] = jnp.zeros((16, LANES), F32)
 
         lane = lax.broadcasted_iota(jnp.int32, (8, LANES), 1)
         first, last = lane == 0, lane == LANES - 1
@@ -250,30 +249,38 @@
                     terms.append(jnp.where(other() > 0.0, face(), dry) if inside else dry)
                 D[flat(x, t), :] = -1.0 - tree(terms)
 
-        arrive(WEIGHT)
-
         def ghost_face(here, other):
             face = scaled_face(here, other)
             return face, jnp.where(other > 0.0, here * (-1.0 / SHIFT) - face, 0.0)
 
-        for side, x, there in ((0, 0, -1), (1, nx - 1, nx)):
-            for t in range(tiles):
-                face, change = ghost_face(B[WEIGHT, at(x, t), :], B[WEIGHT, at(there, t), :])
-                HX[flat((0, nx)[side], t), :] = face
-                D[flat(x, t), :] = D[flat(x, t), :] + change
-        for side in range(2):
-            face, change = ghost_face(B[WEIGHT, y_rows[side], :], YG[WEIGHT, side])
-            HYG[side] = face
-            rows = pl.ds((0, ny - 1)[side], nx, stride=ny)
-            D[rows, :] = D[rows, :] + change
-        ghosts = z_ghost(WEIGHT)
-        changes = []
-        for half in range(halves):
-            face, change = ghost_face(ZS[WEIGHT, half], ghosts[half])
-            FP[half] = face
-            changes.append(change)
-        for x, t in every:
-            D[flat(x, t), :] = D[flat(x, t), :] + unpacked(changes, x, t)
+        def ghost_faces():
+            arrive(WEIGHT)
+            for side, x, there in ((0, 0, -1), (1, nx - 1, nx)):
+                for t in range(tiles):
+                    face, change = ghost_face(B[WEIGHT, at(x, t), :], B[WEIGHT, at(there, t), :])
+                    HX[flat((0, nx)[side], t), :] = face
+                    D[flat(x, t), :] = D[flat(x, t), :] + change
+                    B[1, at(x, t), :] = B[1, at(x, t), :] + change * B[0, at(x, t), :]
+            for side in range(2):
+                face, change = ghost_face(B[WEIGHT, y_rows[side], :], YG[WEIGHT, side])
+                HYG[side] = face
+                rows = pl.ds((0, ny - 1)[side], nx, stride=ny)
+                D[rows, :] = D[rows, :] + change
+                B[1, y_rows[side], :] = B[1, y_rows[side], :] + change * B[0, y_rows[side], :]
+            ghosts = z_ghost(WEIGHT)
+            for half in range(halves):
+                FP[half], CP[half] = ghost_face(ZS[WEIGHT, half], ghosts[half])
+
+        def settle_diagonal():
+            changes = [CP[half] for half in range(halves)]
+            for x, t in every:
+                D[flat(x, t), :] = D[flat(x, t), :] + unpacked(changes, x, t)
+            for half in range(halves):
+                CP[half] = jnp.zeros((8, LANES), F32)
+
+        def keep(k, mixed, square):
+            for offset, value in enumerate((mixed, square)):
+                LS[pl.ds(2 * k + offset, 1), :] = jnp.sum(value.total(), axis=0, keepdims=True)
 
         def moments(k, before):
             mixed, square = Sums(), Sums()
@@ -281,8 +288,7 @@
                 value = B[k, at(x, t), :]
                 mixed.add(value * B[before, at(x, t), :])
                 square.add(value * value)
-            MU[2 * k] = mixed.total()
-            MU[2 * k + 1] = square.total()
+            keep(k, mixed, square)
 
         @pl.loop(0, STEPS)
         def _(k):
@@ -306,8 +312,7 @@
                 square.add(center * center)
                 if not is_rim(x, t):
                     ahead[place(x, t)[0]].add(packed(image, x, t))
-            MU[2 * k] = mixed.total()
-            MU[2 * k + 1] = square.total()
+            keep(k, mixed, square)
             for half in range(halves):
                 ZS[k + 1, half] = ahead[half].total()
 
@@ -318,11 +323,15 @@
                     greet(far.at[round_id + 1], chip_peer(2 << round_id))
                     greet(far.at[round_id + 1], chip_peer(chips - (2 << round_id)))
 
+            @pl.when(k == 0)
+            def _():
+                ghost_faces()
+
             arrive(k)
             for side in range(2):
                 B[k + 1, y_rows[side], :] = B[k + 1, y_rows[side], :] + HYG[side] * YG[k, side]
             ghosts = z_ghost(k)
-            extra = [FP[half] * ghosts[half] for half in range(halves)]
+            extra = [FP[half] * ghosts[half] + CP[half] * ZS[k, half] for half in range(halves)]
             rim = [Sums() for _ in range(halves)]
             for x, t in caps:
                 face, there = (0, -1) if x == 0 else (nx, nx)
@@ -349,9 +358,13 @@
             for x, t in inner:
                 B[k + 1, at(x, t), :] = B[k + 1, at(x, t), :] + unpacked(extra, x, t)
 
+            @pl.when(k == 0)
+            def _():
+                settle_diagonal()
+
         moments(STEPS, STEPS - 1)
 
-        local = jnp.sum(jnp.sum(MU[...], axis=1), axis=1, keepdims=True)
+        local = jnp.sum(LS[...], axis=1, keepdims=True)
         diagonal = (lax.broadcasted_iota(jnp.int32, (16, LANES), 0)
                     == lax.broadcasted_iota(jnp.int32, (16, LANES), 1))
         line = jnp.sum(jnp.where(diagonal, jnp.broadcast_to(local, (16, LANES)), 0.0), axis=0, keepdims=True)
@@ -374,16 +387,21 @@
         def far_known():
             pl.semaphore_wait(far.at[2], 2)
 
+        def hops(count, d):
+            return min(d, count - d)
+
         plane_peers = []
         for c in range(2):
             for dy in range(gyn):
                 for dz in range(gzn):
                     if c or dy or dz:
-                        plane_peers.append({
+                        plane_peers.append((hops(gyn, dy) + hops(gzn, dz), {
                             "gx": gx + 1 - 2 * core if c else gx,
-                            "gy": (gy + dy) % gyn, "gz": (gz + dz) % gzn})
+                            "gy": (gy + dy) % gyn, "gz": (gz + dz) % gzn}))
+        plane_peers = [peer for _, peer in sorted(plane_peers, key=lambda pair: -pair[0])]
+        chip_steps = sorted(range(1, chips), key=lambda d: -hops(chips, d))
         line = all_sum(line, SA, RA, a_send, a_recv, core + 2 * (gy + gyn * gz), plane_peers, far_known)
-        line = all_sum(line, SB, RB, b_send, b_recv, chip, [chip_peer(d) for d in range(1, chips)], drain_halos)
+        line = all_sum(line, SB, RB, b_send, b_recv, chip, [chip_peer(d) for d in chip_steps], drain_halos)
 
         spread = jnp.broadcast_to(line, (8, LANES))
         mu = [jnp.broadcast_to(spread[:, i + 1 : i + 2], (8, LANES)) for i in range(MOMENTS)]
@@ -411,6 +429,16 @@
             scaled[i] = -leftover[i + 1] - scaled[i + 1]
         weights = [value * (1.0 / SHIFT) for value in scaled]
 
+        for i, value in enumerate(weights + leftover):
+            FACTORS[i] = value
+        for landed, sent, count in ((RA, a_send, plane), (RB, b_send, chips)):
+            others = landed.at[pl.ds(0, count - 1)]
+            pltpu.make_async_copy(others, others, sent).wait()
+
+    def combine(B, FACTORS, sol, res, OS, OR, out_sem):
+        weights = [FACTORS[i] for i in range(STEPS)]
+        leftover = [FACTORS[STEPS + i] for i in range(SIZE)]
+
         def out_copies(part):
             where = pl.ds(part * chunk, chunk)
             return [pltpu.make_async_copy(src.at[where], dst.at[where], out_sem.at[i, part])
@@ -429,49 +457,57 @@
             for copy in out_copies(part):
                 copy.start()
 
-        for landed, sent, count in ((RA, a_send, plane), (RB, b_send, chips)):
-            others = landed.at[pl.ds(0, count - 1)]
-            pltpu.make_async_copy(others, others, sent).wait()
-
         @pl.loop(0, nx // chunk)
         def _(part):
             for copy in out_copies(part):
                 copy.wait()
 
+    results = (jax.ShapeDtypeStruct((8, (nx + 2) * pitch, LANES), F32),
+               jax.ShapeDtypeStruct((MOMENTS, 8, LANES), F32))
+    outs = [pltpu.VMEM((nx, ny, nz), F32), pltpu.VMEM((nx, ny, nz), F32),
+            pltpu.SemaphoreType.DMA((2, nx // chunk))]
     scratch = [
         pltpu.VMEM((nx, ny, nz), F32), pltpu.VMEM((nx, ny, nz), F32), pltpu.VMEM((nx, ny, nz), jnp.int32),
-        pltpu.VMEM((8, (nx + 2) * pitch, LANES), F32),
         pltpu.VMEM((8, 2, nx, LANES), F32), pltpu.VMEM((8, 2, nx, LANES), F32),
         pltpu.VMEM((8, halves, 8, LANES), F32), pltpu.VMEM((8, 2, halves, 8, LANES), F32),
         pltpu.VMEM(((nx + 1) * ny, LANES), F32), pltpu.VMEM(((nx + 2) * pitch, LANES), F32),
         pltpu.VMEM((2, nx, LANES), F32),
         pltpu.VMEM((nx * ny, LANES), F32), pltpu.VMEM((nx * ny, LANES), F32),
-        pltpu.VMEM((halves, 8, LANES), F32),
+        pltpu.VMEM((halves, 8, LANES), F32), pltpu.VMEM((halves, 8, LANES), F32),
         pltpu.VMEM((nx * ny, LANES), F32),
-        pltpu.VMEM((16, 8, LANES), F32),
+        pltpu.VMEM((16, LANES), F32),
         pltpu.VMEM((1, LANES), F32), pltpu.VMEM((plane, 1, LANES), F32),
         pltpu.VMEM((1, LANES), F32), pltpu.VMEM((chips, 1, LANES), F32),
-        pltpu.VMEM((nx, ny, nz), F32), pltpu.VMEM((nx, ny, nz), F32),
-        pltpu.SemaphoreType.DMA((3, nx // chunk)), pltpu.SemaphoreType.DMA((2, nx // chunk)),
+        pltpu.SemaphoreType.DMA((3, nx // chunk)),
     ] + [pltpu.SemaphoreType.DMA((8, 2))] * 6 + [pltpu.SemaphoreType.DMA] * 4 + [
         pltpu.SemaphoreType.REGULAR((3,))]
-    return kernel, scratch
+    return kernel, results, scratch, combine, outs
 
 
 def solution(mesh):
     counts = tuple(mesh.shape[axis] for axis in ("gx", "gy", "gz"))
 
     def on_device(right_side, inv_density, active):
-        kernel, scratch = make_kernel(right_side.shape, counts)
+        kernel, results, scratch, combine, outs = make_kernel(right_side.shape, counts)
+        whole = pl.BlockSpec(memory_space=pltpu.VMEM)
+        basis, factors = pl.pallas_call(
+            kernel,
+            out_shape=results,
+            in_specs=[pl.BlockSpec(memory_space=pltpu.HBM)] * 3,
+            out_specs=(whole, whole),
+            scratch_shapes=scratch,
+            compiler_params=pltpu.CompilerParams(
+                collective_id=0, has_side_effects=True, vmem_limit_bytes=16 << 20),
+        )(right_side, inv_density, active)
         field = jax.ShapeDtypeStruct(right_side.shape, F32)
         return pl.pallas_call(
-            kernel,
+            combine,
             out_shape=(field, field),
-            in_specs=[pl.BlockSpec(memory_space=pl.ANY)] * 3,
-            out_specs=(pl.BlockSpec(memory_space=pl.ANY),) * 2,
-            scratch_shapes=scratch,
-            compiler_params=pltpu.CompilerParams(collective_id=0, has_side_effects=True),
-        )(right_side, inv_density, active)
+            in_specs=[whole, whole],
+            out_specs=(pl.BlockSpec(memory_space=pltpu.HBM),) * 2,
+            scratch_shapes=outs,
+            compiler_params=pltpu.CompilerParams(vmem_limit_bytes=16 << 20),
+        )(basis, factors)
 
     placed = P("gx", "gy", "gz")
     return jax.shard_map(

time: 52.1 us -> 53.4 us (1.025)
  Pallas kernels: 48.6 us -> 49.4 us
    pallas_call x1 -> x2, Pallas kernels: 48.6 us -> 49.4 us  [the longest x1 48.2 us: on_device(): pl.pallas_call(kernel, out_shape=results, in_specs=[pl.BlockSpec(memory_s...]
    unnamed x4 -> x6, local copies, waits for them, and re-layouts: 2.74 us -> 3.12 us
where the time goes in v3:
time: 53.4 us; the launch traced here: 53.1 us
  Pallas kernels  49.4 us (93%)
  local copies, waits for them, and re-layouts  3.12 us (6%)
  between operations  0.65 us (1%)
    pallas_call x1, Pallas kernels, on_device(): pl.pallas_call(kernel, out_shape=results, in_specs=[pl.BlockSpec(memory_s...  48.2 us
    unnamed x6, local copies, waits for them, and re-layouts  3.12 us
    pallas_call x1, Pallas kernels, on_device(): pl.pallas_call(combine, out_shape=(field, field), in_specs=[whole, whole]...  1.19 us

profile of v3, /device:TPU:1, one launch (start us, length us, event | category | flops | bytes accessed | tf_op | source)
XLA Modules:
  0.0 53.1 jit_solution(15516854212160255509)
XLA Ops:
  0.6 0.0 copy-start
  0.6 1.0 %copy-done = f32[16,64,128]{2,1,0:T(8,128)S(1)} copy-done((f32[16,64,128]{2,1,0:T(8,128)S(1)}, f32[16,64,128]{2,1,0:T(8,128)}, u32[]{:S(2)}) %copy-start) | copy-done | bytes 524312
  1.7 0.0 copy-start.1
  1.7 1.0 %copy-done.1 = f32[16,64,128]{2,1,0:T(8,128)S(1)} copy-done((f32[16,64,128]{2,1,0:T(8,128)S(1)}, f32[16,64,128]{2,1,0:T(8,128)}, u32[]{:S(2)}) %copy-start.1) | copy-done | bytes 524312
  2.7 0.0 copy-start.2
  2.7 1.0 %copy-done.2 = s32[16,64,128]{2,1,0:T(8,128)S(1)} copy-done((s32[16,64,128]{2,1,0:T(8,128)S(1)}, s32[16,64,128]{2,1,0:T(8,128)}, u32[]{:S(2)}) %copy-start.2) | copy-done | bytes 524312
  3.8 48.2 %shard_map.50 = (f32[8,1440,128]{2,1,0:T(8,128)S(1)}, f32[13,8,128]{2,1,0:T(8,128)S(1)}) custom-call(f32[16,64,128]{2,1,0:T(8,128)S(1)} %copy-done, f32[16,64,128]{2,1,0:T(8,128)S(1)} %copy-done.1, s32[16,64,128]{2,1,0:T(8,128)S(1)} %copy-done.2), custom_call_target="tpu_custom_call" | custom-call | tf_op jit(solution)/shard_map/pallas_call | solution.py:493
  51.9 1.2 %shard_map.51 = (f32[16,64,128]{2,1,0:T(8,128)}, f32[16,64,128]{2,1,0:T(8,128)}) custom-call(f32[8,1440,128]{2,1,0:T(8,128)S(1)} %get-tuple-element.4.B, f32[13,8,128]{2,1,0:T(8,128)S(1)} %get-tuple-element.5.FACTORS), custom_call_target="tpu_custom_call" | custom-call | tf_op jit(solution)/shard_map/pallas_call | solution.py:503
Async XLA Ops:
  0.6 1.0 %copy-start = (f32[16,64,128]{2,1,0:T(8,128)S(1)}, f32[16,64,128]{2,1,0:T(8,128)}, u32[]{:S(2)}) copy-start(f32[16,64,128]{2,1,0:T(8,128)} %rs.1) | copy-start | bytes 1572868
  1.7 1.0 %copy-start.1 = (f32[16,64,128]{2,1,0:T(8,128)S(1)}, f32[16,64,128]{2,1,0:T(8,128)}, u32[]{:S(2)}) copy-start(f32[16,64,128]{2,1,0:T(8,128)} %inv.1) | copy-start | bytes 1572868
  2.7 1.0 %copy-start.2 = (s32[16,64,128]{2,1,0:T(8,128)S(1)}, s32[16,64,128]{2,1,0:T(8,128)}, u32[]{:S(2)}) copy-start(s32[16,64,128]{2,1,0:T(8,128)} %act.1) | copy-start | bytes 1572868

commit v4 on v3

--- a/solution.py
+++ b/solution.py
@@ -498,7 +498,7 @@
             scratch_shapes=scratch,
             compiler_params=pltpu.CompilerParams(
                 collective_id=0, has_side_effects=True, vmem_limit_bytes=16 << 20),
-        )(right_side, inv_density, active)
+        )(*[pltpu.with_memory_space_constraint(a, pltpu.HBM) for a in (right_side, inv_density, active)])
         field = jax.ShapeDtypeStruct(right_side.shape, F32)
         return pl.pallas_call(
             combine,

time: 53.4 us -> 48.3 us (0.904)
  local copies, waits for them, and re-layouts: 3.12 us -> 0 us
  Pallas kernels: 49.4 us -> 47.5 us
    unnamed x6 -> x0, local copies, waits for them, and re-layouts: 3.12 us -> none
    pallas_call x1, Pallas kernels: 48.2 us -> 46.3 us  [on_device(): pl.pallas_call(kernel, out_shape=results, in_specs=[pl.BlockSpec(memory_s...]
where the time goes in v4:
time: 48.3 us; the launch traced here: 48.1 us
  Pallas kernels  47.5 us (98%)
  between operations  0.64 us (1%)
    pallas_call x1, Pallas kernels, on_device(): pl.pallas_call(kernel, out_shape=results, in_specs=[pl.BlockSpec(memory_s...  46.3 us
    pallas_call x1, Pallas kernels, on_device(): pl.pallas_call(combine, out_shape=(field, field), in_specs=[whole, whole]...  1.19 us

profile of v4, /device:TPU:1, one launch (start us, length us, event | category | flops | bytes accessed | tf_op | source)
XLA Modules:
  0.0 48.1 jit_solution(8085355466053066177)
XLA Ops:
  0.6 46.3 %shard_map.50 = (f32[8,1440,128]{2,1,0:T(8,128)S(1)}, f32[13,8,128]{2,1,0:T(8,128)S(1)}) custom-call(f32[16,64,128]{2,1,0:T(8,128)} %rs.1, f32[16,64,128]{2,1,0:T(8,128)} %inv.1, s32[16,64,128]{2,1,0:T(8,128)} %act.1), custom_call_target="tpu_custom_call" | custom-call | tf_op jit(solution)/shard_map/pallas_call | solution.py:493
  46.9 1.2 %shard_map.51 = (f32[16,64,128]{2,1,0:T(8,128)}, f32[16,64,128]{2,1,0:T(8,128)}) custom-call(f32[8,1440,128]{2,1,0:T(8,128)S(1)} %get-tuple-element.4.B, f32[13,8,128]{2,1,0:T(8,128)S(1)} %get-tuple-element.5.FACTORS), custom_call_target="tpu_custom_call" | custom-call | tf_op jit(solution)/shard_map/pallas_call | solution.py:503

commit v5 on v4

--- a/solution.py
+++ b/solution.py
@@ -151,6 +151,11 @@
         first, last = lane == 0, lane == LANES - 1
         ends = first | last
         odd = lane % 2 == 1
+        middle = []
+        for half in range(halves):
+            index = half * (LANES // 2) + ((lane + 1) % LANES) // 2
+            x_at, t_at = index // tiles, index % tiles
+            middle.append((x_at > 0) & (x_at < nx - 1) & (t_at > 0) & (t_at < tiles - 1))
 
         def x_copy(k, side):
             src, dst = ((0, nx), (nx - 1, -1))[side]
@@ -327,28 +332,35 @@
             def _():
                 ghost_faces()
 
-            arrive(k)
+            arrive(k, (1, 2))
             for side in range(2):
                 B[k + 1, y_rows[side], :] = B[k + 1, y_rows[side], :] + HYG[side] * YG[k, side]
             ghosts = z_ghost(k)
             extra = [FP[half] * ghosts[half] + CP[half] * ZS[k, half] for half in range(halves)]
+            for x, t in caps:
+                B[k + 1, at(x, t), :] = B[k + 1, at(x, t), :] + unpacked(extra, x, t)
             rim = [Sums() for _ in range(halves)]
+            for x, t in sides_y:
+                value = B[k + 1, at(x, t), :] + unpacked(extra, x, t)
+                B[k + 1, at(x, t), :] = value
+                rim[place(x, t)[0]].add(packed(value, x, t))
+            for half in range(halves):
+                ZS[k + 1, half] = ZS[k + 1, half] + (rim[half].total() + jnp.where(middle[half], extra[half], 0.0))
+
+            arrive(k, (0,))
+            cap = [Sums() for _ in range(halves)]
             for x, t in caps:
                 face, there = (0, -1) if x == 0 else (nx, nx)
                 value = B[k + 1, at(x, t), :] + HX[flat(face, t), :] * B[k, at(there, t), :]
-                rim[place(x, t)[0]].add(packed(value, x, t))
-                B[k + 1, at(x, t), :] = value + unpacked(extra, x, t)
+                B[k + 1, at(x, t), :] = value
+                cap[place(x, t)[0]].add(packed(value, x, t))
 
             @pl.when(k < STEPS - 1)
             def _():
                 send(k + 1, (0,))
 
-            for x, t in sides_y:
-                value = B[k + 1, at(x, t), :]
-                rim[place(x, t)[0]].add(packed(value, x, t))
-                B[k + 1, at(x, t), :] = value + unpacked(extra, x, t)
             for half in range(halves):
-                ZS[k + 1, half] = ZS[k + 1, half] + (rim[half].total() + extra[half])
+                ZS[k + 1, half] = ZS[k + 1, half] + cap[half].total()
 
             @pl.when(k < STEPS - 1)
             def _():

time: 48.3 us -> 47.5 us (0.983)
  Pallas kernels: 47.5 us -> 46.8 us
    pallas_call x1, Pallas kernels: 46.3 us -> 45.6 us  [on_device(): pl.pallas_call(kernel, out_shape=results, in_specs=[pl.BlockSpec(memory_s...]
where the time goes in v5:
time: 47.5 us; the launch traced here: 47.4 us
  Pallas kernels  46.8 us (99%)
  between operations  0.64 us (1%)
    pallas_call x1, Pallas kernels, on_device(): pl.pallas_call(kernel, out_shape=results, in_specs=[pl.BlockSpec(memory_s...  45.6 us
    pallas_call x1, Pallas kernels, on_device(): pl.pallas_call(combine, out_shape=(field, field), in_specs=[whole, whole]...  1.19 us

profile of v5, /device:TPU:1, one launch (start us, length us, event | category | flops | bytes accessed | tf_op | source)
XLA Modules:
  0.0 47.4 jit_solution(10295431723296190754)
XLA Ops:
  0.6 45.6 %shard_map.50 = (f32[8,1440,128]{2,1,0:T(8,128)S(1)}, f32[13,8,128]{2,1,0:T(8,128)S(1)}) custom-call(f32[16,64,128]{2,1,0:T(8,128)} %rs.1, f32[16,64,128]{2,1,0:T(8,128)} %inv.1, s32[16,64,128]{2,1,0:T(8,128)} %act.1), custom_call_target="tpu_custom_call" | custom-call | tf_op jit(solution)/shard_map/pallas_call | solution.py:505
  46.2 1.2 %shard_map.51 = (f32[16,64,128]{2,1,0:T(8,128)}, f32[16,64,128]{2,1,0:T(8,128)}) custom-call(f32[8,1440,128]{2,1,0:T(8,128)S(1)} %get-tuple-element.4.B, f32[13,8,128]{2,1,0:T(8,128)S(1)} %get-tuple-element.5.FACTORS), custom_call_target="tpu_custom_call" | custom-call | tf_op jit(solution)/shard_map/pallas_call | solution.py:515

commit v6 on v5

--- a/solution.py
+++ b/solution.py
@@ -95,10 +95,6 @@
             return [pltpu.make_async_copy(src.at[where], dst.at[where], in_sem.at[i, part])
                     for i, (src, dst) in enumerate(((rs, rs_v), (inv, inv_v), (act, act_v)))]
 
-        for part in range(nx // chunk):
-            for copy in load_copies(part):
-                copy.start()
-
         low = (gx > 0, gy > 0, gz > 0)
         high = (gx < gxn - 1, gy < gyn - 1, gz < gzn - 1)
         names = ("gx", "gy", "gz")
@@ -123,6 +119,12 @@
 
         greet(barrier, chip_peer(1))
         greet(barrier, chip_peer(chips - 1))
+
+        outside = (0, nx // chunk - 1)
+        order = outside + tuple(part for part in range(nx // chunk) if part not in outside)
+        for part in order:
+            for copy in load_copies(part):
+                copy.start()
 
         for side, there in ((0, low), (1, high)):
             @pl.when(jnp.logical_not(there[0]))
@@ -205,10 +207,10 @@
             return [jnp.where(odd, turn(ZG[k, 1, half], -1), turn(ZG[k, 0, half], 1))
                     for half in range(halves)]
 
-        for part in range(nx // chunk):
+        sums = {}
+        for part in order:
             for copy in load_copies(part):
                 copy.wait()
-            sums = {}
             for x in range(part * chunk, (part + 1) * chunk):
                 for t in range(tiles):
                     rows = pl.ds(8 * t, 8)
@@ -218,15 +220,17 @@
                     B[0, at(x, t), :] = b
                     half = place(x, t)[0]
                     for k, value in ((WEIGHT, w), (0, b)):
-                        sums.setdefault((k, half), Sums()).add(packed(value, x, t))
-            for (k, half), total in sums.items():
-                begins = place(part * chunk, 0)[1] == 0
-                ZS[k, half] = total.total() if begins else ZS[k, half] + total.total()
+                        sums.setdefault((k, half), Sums(2)).add(packed(value, x, t))
+            if part == outside[-1]:
+                pl.semaphore_wait(barrier, present)
+                send(WEIGHT, (0,))
+                send(0, (0,))
+        for (k, half), total in sums.items():
+            ZS[k, half] = total.total()
         y_pack(WEIGHT)
         y_pack(0)
-        pl.semaphore_wait(barrier, present)
-        send(WEIGHT, (0, 1, 2))
-        send(0, (0, 1, 2))
+        send(WEIGHT, (2, 1))
+        send(0, (2, 1))
         greet(far.at[0], chip_peer(1))
         greet(far.at[0], chip_peer(chips - 1))
 
@@ -447,19 +451,21 @@
             others = landed.at[pl.ds(0, count - 1)]
             pltpu.make_async_copy(others, others, sent).wait()
 
+    portion = 4
+
     def combine(B, FACTORS, sol, res, OS, OR, out_sem):
         weights = [FACTORS[i] for i in range(STEPS)]
         leftover = [FACTORS[STEPS + i] for i in range(SIZE)]
 
         def out_copies(part):
-            where = pl.ds(part * chunk, chunk)
+            where = pl.ds(part * portion, portion)
             return [pltpu.make_async_copy(src.at[where], dst.at[where], out_sem.at[i, part])
                     for i, (src, dst) in enumerate(((OS, sol), (OR, res)))]
 
-        @pl.loop(0, nx // chunk)
+        @pl.loop(0, nx // portion)
         def _(part):
-            for within in range(chunk):
-                x = part * chunk + within
+            for within in range(portion):
+                x = part * portion + within
                 for t in range(tiles):
                     where = pl.ds(pl.multiple_of((x + 1) * pitch + 8 + 8 * t, 8), 8)
                     values = [B[i, where, :] for i in range(SIZE)]
@@ -469,7 +475,7 @@
             for copy in out_copies(part):
                 copy.start()
 
-        @pl.loop(0, nx // chunk)
+        @pl.loop(0, nx // portion)
         def _(part):
             for copy in out_copies(part):
                 copy.wait()
@@ -477,7 +483,7 @@
     results = (jax.ShapeDtypeStruct((8, (nx + 2) * pitch, LANES), F32),
                jax.ShapeDtypeStruct((MOMENTS, 8, LANES), F32))
     outs = [pltpu.VMEM((nx, ny, nz), F32), pltpu.VMEM((nx, ny, nz), F32),
-            pltpu.SemaphoreType.DMA((2, nx // chunk))]
+            pltpu.SemaphoreType.DMA((2, nx // portion))]
     scratch = [
         pltpu.VMEM((nx, ny, nz), F32), pltpu.VMEM((nx, ny, nz), F32), pltpu.VMEM((nx, ny, nz), jnp.int32),
         pltpu.VMEM((8, 2, nx, LANES), F32), pltpu.VMEM((8, 2, nx, LANES), F32),

time: 47.5 us -> 47.3 us (level)
  no operation moved by 1% of the time
where the time goes in v6:
time: 47.3 us; the launch traced here: 47.2 us
  Pallas kernels  46.6 us (99%)
  between operations  0.64 us (1%)
    pallas_call x1, Pallas kernels, on_device(): pl.pallas_call(kernel, out_shape=results, in_specs=[pl.BlockSpec(memory_s...  45.4 us
    pallas_call x1, Pallas kernels, on_device(): pl.pallas_call(combine, out_shape=(field, field), in_specs=[whole, whole]...  1.19 us

profile of v6, /device:TPU:1, one launch (start us, length us, event | category | flops | bytes accessed | tf_op | source)
XLA Modules:
  0.0 47.2 jit_solution(17613042181519073468)
XLA Ops:
  0.6 45.4 %shard_map.50 = (f32[8,1440,128]{2,1,0:T(8,128)S(1)}, f32[13,8,128]{2,1,0:T(8,128)S(1)}) custom-call(f32[16,64,128]{2,1,0:T(8,128)} %rs.1, f32[16,64,128]{2,1,0:T(8,128)} %inv.1, s32[16,64,128]{2,1,0:T(8,128)} %act.1), custom_call_target="tpu_custom_call" | custom-call | tf_op jit(solution)/shard_map/pallas_call | solution.py:511
  46.0 1.2 %shard_map.51 = (f32[16,64,128]{2,1,0:T(8,128)}, f32[16,64,128]{2,1,0:T(8,128)}) custom-call(f32[8,1440,128]{2,1,0:T(8,128)S(1)} %get-tuple-element.4.B, f32[13,8,128]{2,1,0:T(8,128)S(1)} %get-tuple-element.5.FACTORS), custom_call_target="tpu_custom_call" | custom-call | tf_op jit(solution)/shard_map/pallas_call | solution.py:521
